TPU v7x, 1024 devices: a whole 4x8x16 slice. The times are simulated.
1024 devices in a mesh: lev: 16 (over x_lo, y), lat: 64 (over z, x_hi, core).
Axes of the slice: x: 4 (x_hi: 2, x_lo: 2; x = x_hi * 2 + x_lo), y: 8, z: 16, core: 2. Of those that a mesh axis runs over, the one named last changes fastest.
Arguments:
- state: float32 [4, 128, 192, 1024], P(None, 'lev', 'lat'), may hold values from -6 to 6
- wind_east: float32 [128, 192, 1024], P('lev', 'lat'), may hold values from -0.45 to 0.45
- wind_north: float32 [128, 192, 1024], P('lev', 'lat'), may hold values from -0.45 to 0.45
- remap_weight: float32 [128, 128], replicated, may hold values from 0.05 to 1
- block_list: int32 [16, 64, 8], P('lev', 'lat'), may hold values from 0 to 7, as said below
- block_count: int32 [16, 64], P('lev', 'lat'), may hold values from 0 to 8, as said below
- w_in: bfloat16 [512, 1024], replicated, may hold values from -1 to 1
- w_mid: bfloat16 [1024, 1024], replicated, may hold values from -0.1875 to 0.1875
- w_out: bfloat16 [1024, 512], replicated, may hold values from -0.375 to 0.375
Outputs:
- new_state: float32 [4, 128, 192, 1024], P(None, 'lev', 'lat')
Inputs may be any that keep to these rules, and one draw needn't show every extreme that they name: Each row block_list[m, g, :] names every block 0 to 7 exactly once. block_count[m, g] + block_count[m, (g + 32) mod 64] equals 8 for every m and g; some entry equals 8.
All inputs are finite; a program needn't handle non-finite values.
Results may differ from a plain program's by a relative error of at most 0.0045.
Values may be sent and summed in bfloat16 or wider, within the bound.
No kernel may reach another device: no remote copies, remote signals or barrier semaphores. Data moves between devices by JAX's collectives and lax.ppermute only.
A program may use at most 32 MiB of HBM per device.

v0:
```python
import jax
import jax.numpy as jnp
from jax import lax
from jax.sharding import PartitionSpec as P

NB = 8


def padded_2(cells, sides, width):
    for axis, dim in sides:
        count = lax.axis_size(axis)
        ends = count - 1
        head = lax.slice_in_dim(cells, 0, width, axis=dim)
        tail = lax.slice_in_dim(cells, cells.shape[dim] - width, cells.shape[dim], axis=dim)
        cells = jnp.concatenate(
            [
                lax.ppermute(tail, axis, [(i, (i + 1) % count) for i in range(ends)]),
                cells,
                lax.ppermute(head, axis, [((i + 1) % count, i) for i in range(ends)]),
            ],
            axis=dim,
        )
    return cells


def remap_matrix(remap_weight):
    identity = jnp.eye(remap_weight.shape[0], dtype=remap_weight.dtype)
    raw_weight = remap_weight + 16.0 * identity
    return raw_weight / jnp.sum(raw_weight, axis=1, keepdims=True)


def physics(blocks, w_in, w_mid, w_out):
    inputs = blocks.reshape(-1, blocks.shape[2])
    first = jax.nn.silu(jnp.dot(inputs, w_in, preferred_element_type=jnp.float32)).astype(
        jnp.bfloat16
    )
    second = jax.nn.silu(jnp.dot(first, w_mid, preferred_element_type=jnp.float32)).astype(
        jnp.bfloat16
    )
    return jnp.dot(second, w_out, preferred_element_type=jnp.float32).reshape(blocks.shape)


def per_device(
    state, wind_east, wind_north, remap_weight, block_list, block_count, w_in, w_mid, w_out
):
    fields, lev_dev, lat_rows, lon_cells = state.shape
    lev_count = lax.axis_size("lev")
    levels = lev_dev * lev_count
    width_in = fields * levels
    global_row = lax.axis_index("lat") * lat_rows + lax.broadcasted_iota(
        jnp.int32, wind_north.shape, 1
    )
    total_rows = lat_rows * lax.axis_size("lat")
    northward = jnp.where(global_row == total_rows - 1, jnp.zeros_like(wind_north), wind_north)
    stacked = jnp.concatenate([state, northward[None]], axis=0)
    padded = padded_2(stacked, (("lat", 2),), 1)
    padded_fields = padded[:fields]
    padded_north = padded[fields]
    face_flux = (
        jnp.maximum(padded_north[:, :-1], 0.0) * padded_fields[:, :, :-1]
        + jnp.minimum(padded_north[:, :-1], 0.0) * padded_fields[:, :, 1:]
    )
    north_south = face_flux[:, :, 1:] - face_flux[:, :, :-1]
    east_cells = jnp.roll(state, -1, axis=3)
    east_flux = jnp.maximum(wind_east, 0.0) * state + jnp.minimum(wind_east, 0.0) * east_cells
    west_flux = jnp.roll(east_flux, 1, axis=3)
    updated = state - (east_flux - west_flux) - north_south
    flat_cols = updated.reshape(fields, lev_dev, lat_rows * lon_cells)
    col_count = lat_rows * lon_cells // lev_count
    remap = remap_matrix(remap_weight)
    column_data = lax.all_to_all(flat_cols, "lev", split_axis=2, concat_axis=1, tiled=True)
    remapped = jnp.einsum("lk,fkc->cfl", remap, column_data, precision=lax.Precision.HIGHEST)
    block_cols = col_count // NB
    blocks = remapped.reshape(NB, block_cols, width_in)
    inputs = blocks.astype(jnp.bfloat16)
    my_list = block_list.reshape(NB)
    my_count = block_count.reshape(())
    slot_ids = lax.broadcasted_iota(jnp.int32, (NB,), 0)
    keep_slot = (slot_ids < my_count)[:, None, None]
    chosen = jnp.take(inputs, my_list, axis=0)
    results = physics(chosen, w_in, w_mid, w_out)
    slot_results = jnp.where(keep_slot, results, 0.0)
    tendency = jnp.zeros((NB, block_cols, width_in), jnp.float32).at[my_list].set(slot_results)
    finished = remapped + tendency.reshape(col_count, fields, levels)
    level_major = jnp.transpose(finished, (1, 2, 0))
    returned_levels = lax.all_to_all(level_major, "lev", split_axis=1, concat_axis=2, tiled=True)
    return returned_levels.reshape(fields, lev_dev, lat_rows, lon_cells)


def solution(mesh):
    placed = (
        P(None, "lev", "lat", None),
        P("lev", "lat", None),
        P("lev", "lat", None),
        P(),
        P("lev", "lat", None),
        P("lev", "lat"),
        P(),
        P(),
        P(),
    )
    return jax.shard_map(
        per_device,
        mesh=mesh,
        in_specs=placed,
        out_specs=P(None, "lev", "lat", None),
        check_vma=False,
    )
```

profile of v0, /device:TPU:8, one launch (start us, length us, event | category | flops | bytes accessed | tf_op | source)
XLA Modules:
  0.0 99.5 jit_solution(461588754131170431)
XLA Ops:
  0.0 0.0 copy-start
  0.0 0.0 slice-start
  0.0 1.1 %select_bitcast_fusion = f32[1,8,3,1024]{3,1,2,0:T(8,128)S(1)} fusion(f32[8,3,1024]{2,0,1:T(8,128)} %param.11, pred[3]{0:T(512)(128)(4,1)S(1)} %add_compare_fusion), kind=kLoop, calls=%fused_computation.35 | loop fusion | flops 24576 | bytes 196611 | tf_op jit(solution)/shard_map/broadcast_in_dim | solution.py:55
  1.2 1.0 pad_maximum_fusion.8
  2.2 1.7 %collective-permute-start = (f32[5,8,1,1024]{3,1,2,0:T(8,128)S(1)}, f32[5,8,1,1024]{3,1,2,0:T(8,128)S(1)}, u32[]{:S(2)}, u32[]{:S(2)}) collective-permute-start(f32[5,8,1,1024]{3,1,2,0:T(8,128)S(1)} %get-tuple-element.5), channel_id=1, source_target_pairs={{0,1},{1,2},{2,3},{3,4},{4,5},{5,6},{6,7},{7,8},{8,9},{9,10},{10,1... | collective-permute-start | bytes 491528 | tf_op jit(solution)/shard_map/ppermute | solution.py:17
  3.9 1.3 %collective-permute-start.1 = (f32[5,8,1,1024]{3,1,2,0:T(8,128)S(1)}, f32[5,8,1,1024]{3,1,2,0:T(8,128)S(1)}, u32[]{:S(2)}, u32[]{:S(2)}) collective-permute-start(f32[5,8,1,1024]{3,1,2,0:T(8,128)S(1)} %get-tuple-element.6), channel_id=1, source_target_pairs={{1,0},{2,1},{3,2},{4,3},{5,4},{6,5},{7,6},{8,7},{9,8},{10,9},{11,1... | collective-permute-start | bytes 491528 | tf_op jit(solution)/shard_map/ppermute | solution.py:19
  5.2 1.2 %slice.46 = f32[4,8,3,1023]{3,1,2,0:T(8,128)S(1)} slice(f32[4,8,3,1024]{3,1,2,0:T(8,128)} %param.9), slice={[0:4], [0:8], [0:3], [1:1024]} | slice | bytes 785664 | tf_op jit(solution)/shard_map/jit(_roll_static)/slice | solution.py:64
  6.4 0.9 broadcast_maximum_fusion
  7.3 0.0 copy-done.1
  7.3 0.0 slice-done
  7.3 0.1 fusion.7
  7.4 0.1 slice.60
  7.5 0.0 collective-permute-done
  7.5 2.5 %collective-permute-done.1 = f32[5,8,1,1024]{3,1,2,0:T(8,128)S(1)} collective-permute-done((f32[5,8,1,1024]{3,1,2,0:T(8,128)S(1)}, f32[5,8,1,1024]{3,1,2,0:T(8,128)S(1)}, u32[]{:S(2)}, u32[]{:S(2)}) %collective-permute-start.1) | collective-permute-done | bytes 163872 | tf_op jit(solution)/shard_map/ppermute | solution.py:19
  10.1 0.1 fusion.1
  10.1 0.2 fusion.6
  10.3 4.4 %copy.17 = f32[4,8,3,1024]{1,0,3,2:T(4,128)} copy(f32[4,8,3,1024]{3,1,2,0:T(8,128)S(1)} %fusion.6) | data formatting | bytes 786432 | tf_op jit(solution)/shard_map/sub | solution.py:67
  14.8 9.4 %reshape.93 = f32[16,1,6144]{2,1,0:T(1,128)} reshape(f32[3072,4,8]{2,1,0:T(4,128)} %bitcast.48) | data formatting | bytes 786432
  24.1 13.5 %all-to-all-start = ((f32[16,1,6144]{2,1,0:T(1,128)}), f32[16,1,6144]{2,1,0:T(1,128)S(1)}, u32[]{:S(2)}, u32[]{:S(2)}) async-start(f32[16,1,6144]{2,1,0:T(1,128)} %reshape.93), calls=%async_computation | async-start | bytes 786432 | tf_op jit(solution)/shard_map/all_to_all | solution.py:71
  37.6 0.0 copy-done.4
  37.6 0.1 broadcast_in_dim.40
  37.7 0.1 broadcast_in_dim.41
  38.5 0.0 copy-done.3
  38.5 0.1 fusion.15
  38.6 12.1 %all-to-all-done = f32[16,1,6144]{2,1,0:T(1,128)S(1)} async-done(((f32[16,1,6144]{2,1,0:T(1,128)}), f32[16,1,6144]{2,1,0:T(1,128)S(1)}, u32[]{:S(2)}, u32[]{:S(2)}) %all-to-all-start) | async-done | bytes 393248 | tf_op jit(solution)/shard_map/all_to_all | solution.py:71
  50.7 0.5 broadcast.97
  51.2 1.6 %reduce = f32[16,6144]{1,0:T(8,128)S(1)} reduce(f32[16,1,6144]{2,1,0:T(1,128)S(1)} %all-to-all-done, f32[]{:T(128)} %broadcast.97), dimensions={1}, to_apply=%all_to_all.24.reduce_sub_computation | reduce | bytes 786436 | tf_op jit(solution)/shard_map/all_to_all | solution.py:71
  52.7 9.2 %reshape.94 = f32[3072,4,8]{2,1,0:T(4,128)} reshape(f32[16,6144]{1,0:T(8,128)S(1)} %reduce) | data formatting | bytes 786432
  62.0 5.6 %copy.29 = f32[4,8,16,192]{3,1,2,0:T(8,128)S(1)} copy(f32[4,8,16,192]{1,0,3,2:T(4,128)} %bitcast.49) | data formatting | bytes 786432 | tf_op jit(solution)/shard_map/all_to_all | solution.py:71
  67.6 1.8 %fusion.24 = (bf16[192,4,128]{2,0,1:T(8,128)(2,1)S(1)}, f32[192,4,128]{2,0,1:T(8,128)}) fusion(f32[128,128]{1,0:T(8,128)S(1)} %copy-done.3, f32[128]{0:T(128)S(1)} %fusion.15, f32[4,8,16,192]{3,1,2,0:T(8,128)S(1)} %copy.29), kind=kOutput, calls=%fused_computation.56 | convolution fusion | flops 151158784 | bytes 1049088 | tf_op jit(solution)/shard_map/lk,fkc->cfl/dot_general | solution.py:72
  69.3 0.2 copy.21
  69.5 0.1 convert_element_type.14
  69.6 0.6 gather_fusion
  70.1 0.1 bitcast_select_fusion
  70.2 0.3 copy-done.2
  70.6 1.3 %fusion.25 = f32[192,1024]{1,0:T(8,128)} fusion(bf16[192,512]{1,0:T(8,128)(2,1)S(1)} %bitcast_select_fusion, bf16[512,1024]{1,0:T(8,128)(2,1)S(1)} %copy-done.2), kind=kOutput, calls=%fused_computation.57 | convolution fusion | flops 201326592 | bytes 2031616 | tf_op jit(solution)/shard_map/dot_general | solution.py:34
  71.8 0.0 copy-done
  71.8 2.3 %fusion.5 = f32[192,512]{1,0:T(8,128)S(1)} fusion(bf16[1024,512]{1,0:T(8,128)(2,1)} %param.17, bf16[1024,1024]{1,0:T(8,128)(2,1)S(1)} %copy-done, f32[192,1024]{1,0:T(8,128)} %fusion.25), kind=kOutput, calls=%fused_computation.15 | convolution fusion | flops 605945856 | bytes 4325376 | tf_op jit(solution)/shard_map/dot_general | solution.py:40
  74.1 0.1 broadcast_select_fusion
  74.3 0.8 scatter_fusion
  75.1 0.1 reshape.74
  75.2 1.0 %fusion.9 = f32[4,128,192]{1,2,0:T(8,128)S(1)} fusion(f32[192,4,128]{2,0,1:T(8,128)} %get-tuple-element.12, f32[192,4,128]{2,1,0:T(4,128)S(1)} %reshape.74), kind=kLoop, calls=%fused_computation.23 | loop fusion | flops 98304 | bytes 1179648 | tf_op jit(solution)/shard_map/transpose | solution.py:85
  76.3 0.2 copy.23
  76.5 21.2 %all_to_all.33 = f32[4,128,192]{2,0,1:T(4,128)S(1)} all-to-all(f32[4,128,192]{2,0,1:T(4,128)S(1)} %copy.23), channel_id=1, replica_groups=mesh['lev'=16,'lat'=64] {'lev'}, dimensions={1} | all-to-all | bytes 786432 | tf_op jit(solution)/shard_map/all_to_all | solution.py:86
  97.8 0.1 copy.34
  97.9 0.2 copy.25
  98.0 0.4 reshape.75
  98.5 1.0 copy.26
  (12 shorter events, 0.1 us)
Async XLA Ops:
  0.0 71.8 %copy-start = (bf16[1024,1024]{1,0:T(8,128)(2,1)S(1)}, bf16[1024,1024]{1,0:T(8,128)(2,1)}, u32[]{:S(2)}) copy-start(bf16[1024,1024]{1,0:T(8,128)(2,1)} %param.16) | copy-start | bytes 6291460
  0.0 7.3 %copy-start.1 = (f32[4,8,3,1024]{3,1,2,0:T(8,128)S(1)}, f32[4,8,3,1024]{3,1,2,0:T(8,128)}, u32[]{:S(2)}) copy-start(f32[4,8,3,1024]{3,1,2,0:T(8,128)} %param.9) | copy-start | bytes 1179652
  0.0 7.3 %slice-start = ((f32[4,8,3,1024]{3,1,2,0:T(8,128)}), f32[4,8,3,1]{3,1,2,0:T(8,128)S(1)}, s32[]{:S(2)}) async-start(f32[4,8,3,1024]{3,1,2,0:T(8,128)} %param.9), calls=%async_computation.2 | async-start | bytes 98304 | tf_op jit(solution)/shard_map/jit(_roll_static)/slice | solution.py:64
  2.2 5.4 %collective-permute-start = (f32[5,8,1,1024]{3,1,2,0:T(8,128)S(1)}, f32[5,8,1,1024]{3,1,2,0:T(8,128)S(1)}, u32[]{:S(2)}, u32[]{:S(2)}) collective-permute-start(f32[5,8,1,1024]{3,1,2,0:T(8,128)S(1)} %get-tuple-element.5), channel_id=1, source_target_pairs={{0,1},{1,2},{2,3},{3,4},{4,5},{5,6},{6,7},{7,8},{8,9},{9,10},{10,1... | collective-permute-start | bytes 491528 | tf_op jit(solution)/shard_map/ppermute | solution.py:17
  3.9 6.1 %collective-permute-start.1 = (f32[5,8,1,1024]{3,1,2,0:T(8,128)S(1)}, f32[5,8,1,1024]{3,1,2,0:T(8,128)S(1)}, u32[]{:S(2)}, u32[]{:S(2)}) collective-permute-start(f32[5,8,1,1024]{3,1,2,0:T(8,128)S(1)} %get-tuple-element.6), channel_id=1, source_target_pairs={{1,0},{2,1},{3,2},{4,3},{5,4},{6,5},{7,6},{8,7},{9,8},{10,9},{11,1... | collective-permute-start | bytes 491528 | tf_op jit(solution)/shard_map/ppermute | solution.py:19
  14.8 22.8 %copy-start.4 = (s32[1,1,8]{2,1,0:T(1,128)S(1)}, s32[1,1,8]{2,1,0:T(1,128)}, u32[]{:S(2)}) copy-start(s32[1,1,8]{2,1,0:T(1,128)} %param.13) | copy-start | bytes 100
  14.8 23.7 %copy-start.3 = (f32[128,128]{1,0:T(8,128)S(1)}, f32[128,128]{1,0:T(8,128)}, u32[]{:S(2)}) copy-start(f32[128,128]{1,0:T(8,128)} %param.12) | copy-start | bytes 196612
  24.1 26.5 %all-to-all-start = ((f32[16,1,6144]{2,1,0:T(1,128)}), f32[16,1,6144]{2,1,0:T(1,128)S(1)}, u32[]{:S(2)}, u32[]{:S(2)}) async-start(f32[16,1,6144]{2,1,0:T(1,128)} %reshape.93), calls=%async_computation | async-start | bytes 786432 | tf_op jit(solution)/shard_map/all_to_all | solution.py:71
  69.3 1.2 %copy-start.2 = (bf16[512,1024]{1,0:T(8,128)(2,1)S(1)}, bf16[512,1024]{1,0:T(8,128)(2,1)}, u32[]{:S(2)}) copy-start(bf16[512,1024]{1,0:T(8,128)(2,1)} %param.15) | copy-start | bytes 3145732
where the time goes:
time: 100 us; the launch traced here: 99.5 us
  local copies, waits for them, and re-layouts  34.5 us (34%)
  blocking collectives  21.2 us (21%)
  starting transfers between devices  16.5 us (16%)
  waiting for transfers between devices  14.6 us (15%)
  other arithmetic  6.37 us (6%)
  matrix products  5.32 us (5%)
    all_to_all x1, blocking collectives, per_device(): lax.all_to_all(level_major, 'lev', split_axis=1, concat_axis=2, tiled=True)  21.2 us
    unnamed x12, local copies, waits for them, and re-layouts  18.9 us
    all_to_all x1, starting transfers between devices, per_device(): lax.all_to_all(flat_cols, 'lev', split_axis=2, concat_axis=1, tiled=True)  13.5 us
    all_to_all x1, waiting for transfers between devices, per_device(): lax.all_to_all(flat_cols, 'lev', split_axis=2, concat_axis=1, tiled=True)  12.1 us
    all_to_all x2, local copies, waits for them, and re-layouts, per_device(): lax.all_to_all(flat_cols, 'lev', split_axis=2, concat_axis=1, tiled=True)  6.12 us
    sub x1, local copies, waits for them, and re-layouts, per_device(): updated = state - (east_flux - west_flux) - north_south  4.44 us
    ppermute x1, waiting for transfers between devices, padded_2(): lax.ppermute(head, axis, [((i + 1) % count, i) for i in range(ends)])  2.49 us
    dot_general x1, matrix products, physics(): jnp.dot(second, w_out, preferred_element_type=jnp.float32)  2.29 us
  transfers between devices with their start and end apart: 3, of which 2 were waited for; matrix products, arithmetic and copies ran while one was open for 3% of the time, Pallas kernels for 0%

commit v1 on v0

v1 whole, which is shorter than its diff:
```python
import jax
import jax.numpy as jnp
from jax import lax
from jax.experimental import pallas as pl
from jax.experimental.pallas import tpu as pltpu
from jax.sharding import PartitionSpec as P

NB = 8
F32 = jnp.float32
BF16 = jnp.bfloat16
VM = pltpu.VMEM


def whole():
    return pl.BlockSpec(memory_space=VM)


def params(mib):
    return pltpu.CompilerParams(vmem_limit_bytes=mib * 2**20)


def edge_kernel(state_ref, north_ref, up_ref, down_ref):
    fields = state_ref.shape[0]
    for f in range(fields):
        up_ref[f] = state_ref[f, 2].astype(BF16)
        down_ref[f] = state_ref[f, 0].astype(BF16)
    up_ref[fields] = north_ref[2].astype(BF16)


def flux_kernel(state_ref, east_ref, north_ref, south_edge_ref, north_edge_ref, out_ref):
    fields, rows = state_ref.shape[:2]
    last = lax.axis_index("lat") == lax.axis_size("lat") - 1
    keep_wall = jnp.where(last, 0.0, 1.0).astype(F32)
    lane = lax.broadcasted_iota(jnp.int32, (8, 128), 1)
    low = lane < 64
    wind_below = south_edge_ref[fields].astype(F32)
    updated = []
    for f in range(fields):
        cells = [state_ref[f, j] for j in range(rows)]
        above = cells[1:] + [north_edge_ref[f].astype(F32)]
        below_flux = (
            jnp.maximum(wind_below, 0.0) * south_edge_ref[f].astype(F32)
            + jnp.minimum(wind_below, 0.0) * cells[0]
        )
        pieces = []
        for j in range(rows):
            wind = north_ref[j]
            if j == rows - 1:
                wind = wind * keep_wall
            north_flux = jnp.maximum(wind, 0.0) * cells[j] + jnp.minimum(wind, 0.0) * above[j]
            easterly = east_ref[j]
            width = cells[j].shape[1]
            east_cells = pltpu.roll(cells[j], width - 1, 1)
            east_flux = jnp.maximum(easterly, 0.0) * cells[j] + jnp.minimum(easterly, 0.0) * east_cells
            west_flux = pltpu.roll(east_flux, 1, 1)
            pieces.append(cells[j] - (east_flux - west_flux) - (north_flux - below_flux))
            below_flux = north_flux
        updated.append(pieces)

    def tile(f, v):
        j, k = divmod(v, 8)
        return updated[f][j][:, k * 128 : (k + 1) * 128]

    for p in range(8):
        full_a = [tile(f, 3 * p) for f in range(fields)]
        half = [tile(f, 3 * p + 1) for f in range(fields)]
        full_b = [tile(f, 3 * p + 2) for f in range(fields)]
        turned = [pltpu.roll(h, 64, 1) for h in half]
        half_a = [jnp.where(low, half[f], turned[f + 2]) for f in range(2)]
        half_b = [jnp.where(low, turned[f], half[f + 2]) for f in range(2)]
        out_ref[2 * p] = jnp.concatenate(full_a + half_a, axis=0).astype(BF16)
        out_ref[2 * p + 1] = jnp.concatenate(full_b + half_b, axis=0).astype(BF16)


def remap_kernel(weight_ref, high_ref, low_ref):
    n = weight_ref.shape[0]
    row = lax.broadcasted_iota(jnp.int32, (n, n), 0)
    col = lax.broadcasted_iota(jnp.int32, (n, n), 1)
    raw = weight_ref[...] + jnp.where(row == col, 16.0, 0.0)
    remap = (raw / jnp.sum(raw, axis=1, keepdims=True)).T
    zero = jnp.zeros((8, n), F32)
    rows = []
    for m in range(n // 8):
        piece = remap[m * 8 : (m + 1) * 8]
        rows.append(jnp.concatenate([piece, zero], axis=1))
        rows.append(jnp.concatenate([zero, piece], axis=1))
    pair = jnp.concatenate(rows, axis=0)
    high = pair.astype(BF16)
    high_ref[...] = high
    low_ref[...] = (pair - high.astype(F32)).astype(BF16)


def silu(v):
    return v / (1.0 + jnp.exp(-v))


def physics_kernel(list_ref, count_ref, data_ref, high_ref, low_ref, w_in_ref, w_mid_ref, w_out_ref, out_ref):
    bits = jnp.int32(0)
    count = count_ref[0, 0]
    for s in range(NB):
        bits = bits + jnp.where(s < count, jnp.left_shift(jnp.int32(1), list_ref[0, 0, s]), 0)
    odd = lax.rem(lax.axis_index("lev"), 2)

    def turned(r):
        block = data_ref[:, r : r + 16, :].reshape(256, 128)
        return block.T

    ends = turned(32)
    x = []
    for p in range(2):
        cols = jnp.concatenate([turned(16 * p), ends[64 * p : 64 * p + 64]], axis=0)
        x.append(
            jnp.dot(cols, high_ref[...], preferred_element_type=F32)
            + jnp.dot(cols, low_ref[...], preferred_element_type=F32)
        )
    remapped = jnp.concatenate(x, axis=1)
    first = silu(jnp.dot(remapped.astype(BF16), w_in_ref[...], preferred_element_type=F32)).astype(BF16)
    second = silu(jnp.dot(first, w_mid_ref[...], preferred_element_type=F32)).astype(BF16)
    tendency = jnp.dot(second, w_out_ref[...], preferred_element_type=F32)
    place = lax.broadcasted_iota(jnp.int32, tendency.shape, 0)
    column = jnp.where(place < 128, place + 64 * odd, place - 128 * odd)
    block = jnp.right_shift(column * 2731, 16)
    active = jnp.bitwise_and(jnp.right_shift(jnp.full(tendency.shape, bits), block), 1) == 1
    finished = remapped + jnp.where(active, tendency, 0.0)

    def put(r, rows):
        back = rows.T.reshape(2, 16, 8, 128)
        both = jnp.concatenate([back[0], back[1]], axis=1)
        out_ref[:, r : r + 16, :] = both.astype(BF16)

    put(0, finished[:128, :256])
    put(16, finished[:128, 256:])
    put(32, jnp.concatenate([finished[128:, :256], finished[128:, 256:]], axis=0))


def unpack_kernel(data_ref, out_ref):
    fields = out_ref.shape[0]
    lane = lax.broadcasted_iota(jnp.int32, (16, 128), 1)
    low = lane < 64

    def put(v, pair, value):
        j, k = divmod(v, 8)
        for f in range(2):
            out_ref[2 * pair + f, j, :, k * 128 : (k + 1) * 128] = value[8 * f : 8 * f + 8]

    for p in range(8):
        a = data_ref[2 * p].astype(F32)
        b = data_ref[2 * p + 1].astype(F32)
        for pair in range(2):
            put(3 * p, pair, a[16 * pair : 16 * pair + 16])
            put(3 * p + 2, pair, b[16 * pair : 16 * pair + 16])
        end_a, end_b = a[32:], b[32:]
        put(3 * p + 1, 0, jnp.where(low, end_a, pltpu.roll(end_b, 64, 1)))
        put(3 * p + 1, 1, jnp.where(low, pltpu.roll(end_a, 64, 1), end_b))


def per_device(
    state, wind_east, wind_north, remap_weight, block_list, block_count, w_in, w_mid, w_out
):
    fields, lev_dev, lat_rows, lon_cells = state.shape
    lev_count = lax.axis_size("lev")
    lat_count = lax.axis_size("lat")
    cells = jnp.transpose(state, (0, 2, 1, 3))
    east = jnp.transpose(wind_east, (1, 0, 2))
    north = jnp.transpose(wind_north, (1, 0, 2))
    edge = (lev_dev, lon_cells)
    up, down = pl.pallas_call(
        edge_kernel,
        out_shape=[
            jax.ShapeDtypeStruct((fields + 1, *edge), BF16),
            jax.ShapeDtypeStruct((fields, *edge), BF16),
        ],
        in_specs=[whole()] * 2,
        out_specs=[whole()] * 2,
        compiler_params=params(8),
        name="edges",
    )(cells, north)
    south_edge = lax.ppermute(up, "lat", [(i, i + 1) for i in range(lat_count - 1)])
    north_edge = lax.ppermute(down, "lat", [(i + 1, i) for i in range(lat_count - 1)])
    chunk = (lev_count, fields * lev_dev * lat_rows * lon_cells // lev_count // 128, 128)
    packed = pl.pallas_call(
        flux_kernel,
        out_shape=jax.ShapeDtypeStruct(chunk, BF16),
        in_specs=[whole()] * 5,
        out_specs=whole(),
        compiler_params=params(8),
        name="flux",
    )(cells, east, north, south_edge, north_edge)
    levels = lev_dev * lev_count
    high, low = pl.pallas_call(
        remap_kernel,
        out_shape=[jax.ShapeDtypeStruct((2 * levels, 2 * levels), BF16)] * 2,
        in_specs=[whole()],
        out_specs=[whole()] * 2,
        compiler_params=params(8),
        name="remap",
    )(remap_weight)
    columns = lax.all_to_all(packed, "lev", split_axis=0, concat_axis=0, tiled=True)
    smem = pl.BlockSpec(memory_space=pltpu.SMEM)
    finished = pl.pallas_call(
        physics_kernel,
        out_shape=jax.ShapeDtypeStruct(chunk, BF16),
        in_specs=[smem, smem] + [whole()] * 6,
        out_specs=whole(),
        compiler_params=params(24),
        name="physics",
    )(block_list, block_count, columns, high, low, w_in, w_mid, w_out)
    returned = lax.all_to_all(finished, "lev", split_axis=0, concat_axis=0, tiled=True)
    result = pl.pallas_call(
        unpack_kernel,
        out_shape=jax.ShapeDtypeStruct(cells.shape, F32),
        in_specs=[whole()],
        out_specs=whole(),
        compiler_params=params(8),
        name="unpack",
    )(returned)
    return jnp.transpose(result, (0, 2, 1, 3))


def solution(mesh):
    placed = (
        P(None, "lev", "lat", None),
        P("lev", "lat", None),
        P("lev", "lat", None),
        P(),
        P("lev", "lat", None),
        P("lev", "lat"),
        P(),
        P(),
        P(),
    )
    return jax.shard_map(
        per_device,
        mesh=mesh,
        in_specs=placed,
        out_specs=P(None, "lev", "lat", None),
        check_vma=False,
    )
```

time: 100 us -> 54.5 us (0.55)
  local copies, waits for them, and re-layouts: 34.5 us -> 7.09 us
  blocking collectives: 21.2 us -> 13.1 us
  other arithmetic: 6.37 us -> 0 us
  matrix products: 5.32 us -> 0 us
  Pallas kernels: 0 us -> 4.23 us
  waiting for transfers between devices: 14.6 us -> 12.6 us
    unnamed x12 -> x16, local copies, waits for them, and re-layouts: 18.9 us -> 7.09 us
    all_to_all x1, blocking collectives: 21.2 us -> 13.1 us  [per_device(): lax.all_to_all(finished, 'lev', split_axis=0, concat_axis=0, tiled=True)]
    all_to_all x4 -> x0, local copies, waits for them, and re-layouts: 6.39 us -> none  [the longest x2 6.12 us: per_device(): lax.all_to_all(flat_cols, 'lev', split_axis=2, concat_axis=1, tiled=True)]
    dot_general x3 -> x0, matrix products: 5.32 us -> none  [the longest x1 2.29 us: physics(): jnp.dot(second, w_out, preferred_element_type=jnp.float32)]
    sub x1 -> x0, local copies, waits for them, and re-layouts: 4.44 us -> none  [per_device(): updated = state - (east_flux - west_flux) - north_south]
    pallas_call x0 -> x5, Pallas kernels: none -> 4.23 us  [the longest x1 1.91 us: per_device(): pl.pallas_call(physics_kernel, out_shape=jax.ShapeDtypeStruct(chunk, BF16...]
    all_to_all x1, waiting for transfers between devices: 12.1 us -> 7.92 us  [per_device(): lax.all_to_all(packed, 'lev', split_axis=0, concat_axis=0, tiled=True)]
    ppermute x2, waiting for transfers between devices: 2.5 us -> 4.66 us  [the longest x1 4.65 us: per_device(): lax.ppermute(down, 'lat', [(i + 1, i) for i in range(lat_count - 1)])]
  transfers between devices with their start and end apart: 3 -> 3, of which waited for: 2 -> 2; matrix products, arithmetic and copies ran while one was open for 3% -> 0% of each run, Pallas kernels for 0% -> 0%
where the time goes in v1:
time: 54.5 us; the launch traced here: 54 us
  starting transfers between devices  16.3 us (30%)
  blocking collectives  13.1 us (24%)
  waiting for transfers between devices  12.6 us (23%)
  local copies, waits for them, and re-layouts  7.09 us (13%)
  Pallas kernels  4.23 us (8%)
  between operations  0.71 us (1%)
    all_to_all x1, starting transfers between devices, per_device(): lax.all_to_all(packed, 'lev', split_axis=0, concat_axis=0, tiled=True)  13.1 us
    all_to_all x1, blocking collectives, per_device(): lax.all_to_all(finished, 'lev', split_axis=0, concat_axis=0, tiled=True)  13.1 us
    all_to_all x1, waiting for transfers between devices, per_device(): lax.all_to_all(packed, 'lev', split_axis=0, concat_axis=0, tiled=True)  7.92 us
    unnamed x16, local copies, waits for them, and re-layouts  7.09 us
    ppermute x1, waiting for transfers between devices, per_device(): lax.ppermute(down, 'lat', [(i + 1, i) for i in range(lat_count - 1)])  4.65 us
    pallas_call x1, Pallas kernels, per_device(): pl.pallas_call(physics_kernel, out_shape=jax.ShapeDtypeStruct(chunk, BF16...  1.91 us
    ppermute x1, starting transfers between devices, per_device(): lax.ppermute(up, 'lat', [(i, i + 1) for i in range(lat_count - 1)])  1.87 us
    ppermute x1, starting transfers between devices, per_device(): lax.ppermute(down, 'lat', [(i + 1, i) for i in range(lat_count - 1)])  1.29 us
  transfers between devices with their start and end apart: 3, of which 2 were waited for; matrix products, arithmetic and copies ran while one was open for 0% of the time, Pallas kernels for 0%

profile of v1, /device:TPU:8, one launch (start us, length us, event | category | flops | bytes accessed | tf_op | source)
XLA Modules:
  0.0 54.0 jit_solution(10490950017071304365)
XLA Ops:
  0.0 0.0 copy-start.1
  0.0 1.0 %copy-done.1 = f32[4,8,3,1024]{3,1,2,0:T(8,128)S(1)} copy-done((f32[4,8,3,1024]{3,1,2,0:T(8,128)S(1)}, f32[4,8,3,1024]{3,1,2,0:T(8,128)}, u32[]{:S(2)}) %copy-start.1) | copy-done | bytes 393240
  1.0 0.0 copy-start.4
  1.0 0.9 %copy-done.4 = f32[8,3,1024]{2,0,1:T(8,128)S(1)} copy-done((f32[8,3,1024]{2,0,1:T(8,128)S(1)}, f32[8,3,1024]{2,0,1:T(8,128)}, u32[]{:S(2)}) %copy-start.4) | copy-done | bytes 98328
  1.9 0.0 copy-start.2
  1.9 1.9 %collective-permute-start = (bf16[5,8,1024]{2,1,0:T(8,128)(2,1)S(1)}, bf16[5,8,1024]{2,1,0:T(8,128)(2,1)S(1)}, u32[]{:S(2)}, u32[]{:S(2)}) collective-permute-start(bf16[5,8,1024]{2,1,0:T(8,128)(2,1)S(1)} %get-tuple-element.9), channel_id=1, source_target_pairs={{0,1},{1,2},{2,3},{3,4},{4,5},{5,6},{6,7},{7,8},{8,9},{9,10},{10,1... | collective-permute-start | bytes 245768 | tf_op jit(solution)/shard_map/ppermute | solution.py:178
  3.8 1.3 %collective-permute-start.1 = (bf16[4,8,1024]{2,1,0:T(8,128)(2,1)S(1)}, bf16[4,8,1024]{2,1,0:T(8,128)(2,1)S(1)}, u32[]{:S(2)}, u32[]{:S(2)}) collective-permute-start(bf16[4,8,1024]{2,1,0:T(8,128)(2,1)S(1)} %get-tuple-element.10), channel_id=1, source_target_pairs={{1,0},{2,1},{3,2},{4,3},{5,4},{6,5},{7,6},{8,7},{9,8},{10,9},{11,1... | collective-permute-start | bytes 196616 | tf_op jit(solution)/shard_map/ppermute | solution.py:179
  5.1 4.7 %collective-permute-done.1.north_edge_ref = bf16[4,8,1024]{2,1,0:T(8,128)(2,1)S(1)} collective-permute-done((bf16[4,8,1024]{2,1,0:T(8,128)(2,1)S(1)}, bf16[4,8,1024]{2,1,0:T(8,128)(2,1)S(1)}, u32[]{:S(2)}, u32[]{:S(2)}) %collective-permute-start.1) | collective-permute-done | bytes 65568 | tf_op jit(solution)/shard_map/ppermute | solution.py:179
  9.7 0.0 collective-permute-done.south_edge_ref
  9.8 0.0 copy-start.5
  9.8 0.9 %copy-done.5 = f32[8,3,1024]{2,0,1:T(8,128)S(1)} copy-done((f32[8,3,1024]{2,0,1:T(8,128)S(1)}, f32[8,3,1024]{2,0,1:T(8,128)}, u32[]{:S(2)}) %copy-start.5) | copy-done | bytes 98328
  10.6 1.3 %flux.1 = bf16[16,48,128]{2,1,0:T(8,128)(2,1)} custom-call(f32[4,3,8,1024]{3,2,1,0:T(8,128)S(1)} %bitcast.5, f32[3,8,1024]{2,1,0:T(8,128)S(1)} %bitcast.8, f32[3,8,1024]{2,1,0:T(8,128)S(1)} %bitcast.7, bf16[5,8,1024]{2,1,0:T(8,128)(2,1)S(1)} %collective-permute-done.south_edge_ref, bf16[4,8,1024]{2,1,0:T(8,128)(2,1)S(1)} %collective-permute-done.1.north_edge_ref), custom_call_target="tpu_custom_call" | custom-call | tf_op jit(solution)/shard_map/flux/pallas_call | solution.py:181
  11.9 13.1 %all-to-all-start = ((bf16[16,48,128]{2,1,0:T(8,128)(2,1)}), bf16[16,48,128]{2,1,0:T(8,128)(2,1)S(1)}, u32[]{:S(2)}, u32[]{:S(2)}) async-start(bf16[16,48,128]{2,1,0:T(8,128)(2,1)} %flux.1), calls=%async_computation | async-start | bytes 393216 | tf_op jit(solution)/shard_map/all_to_all | solution.py:198
  25.7 0.0 copy-start.6
  25.7 0.8 %copy-done.6 = f32[128,128]{1,0:T(8,128)S(1)} copy-done((f32[128,128]{1,0:T(8,128)S(1)}, f32[128,128]{1,0:T(8,128)}, u32[]{:S(2)}) %copy-start.6) | copy-done | bytes 65560
  26.6 0.2 remap.1
  26.7 7.9 %all-to-all-done.data_ref = bf16[16,48,128]{2,1,0:T(8,128)(2,1)S(1)} async-done(((bf16[16,48,128]{2,1,0:T(8,128)(2,1)}), bf16[16,48,128]{2,1,0:T(8,128)(2,1)S(1)}, u32[]{:S(2)}, u32[]{:S(2)}) %all-to-all-start) | async-done | bytes 196640 | tf_op jit(solution)/shard_map/all_to_all | solution.py:198
  34.7 0.0 copy-done.2
  34.7 0.0 copy-start
  34.7 1.6 %copy-done = bf16[1024,1024]{1,0:T(8,128)(2,1)S(1)} copy-done((bf16[1024,1024]{1,0:T(8,128)(2,1)S(1)}, bf16[1024,1024]{1,0:T(8,128)(2,1)}, u32[]{:S(2)}) %copy-start) | copy-done | bytes 2097176
  36.3 0.0 copy-start.3
  36.3 1.2 %copy-done.3 = bf16[1024,512]{1,0:T(8,128)(2,1)S(1)} copy-done((bf16[1024,512]{1,0:T(8,128)(2,1)S(1)}, bf16[1024,512]{1,0:T(8,128)(2,1)}, u32[]{:S(2)}) %copy-start.3) | copy-done | bytes 1048600
  37.5 0.0 copy-start.7
  37.5 0.7 %copy-done.7 = s32[1,1,8]{2,1,0:T(1,128)S(1)} copy-done((s32[1,1,8]{2,1,0:T(1,128)S(1)}, s32[1,1,8]{2,1,0:T(1,128)}, u32[]{:S(2)}) %copy-start.7) | copy-done | bytes 56
  38.1 1.9 %physics.1 = bf16[16,48,128]{2,1,0:T(8,128)(2,1)S(1)} custom-call(s32[1,1,8]{2,1,0:T(1,128)S(1)} %copy-done.7, s32[1,1]{1,0:T(1,128)S(6)} %copy.10.count_ref, bf16[16,48,128]{2,1,0:T(8,128)(2,1)S(1)} %all-to-all-done.data_ref, bf16[256,256]{1,0:T(8,128)(2,1)S(1)} %get-tuple-element.11.high_ref, bf16[256,256]{1,0:T(8,128)(2,1)S(1)} %get-tuple-element.12.low_ref, ...), custom_call_target="tpu_custom_call" | custom-call | tf_op jit(solution)/shard_map/physics/pallas_call | solution.py:200
  40.1 13.1 %all_to_all.10.data_ref = bf16[16,48,128]{2,1,0:T(8,128)(2,1)S(1)} all-to-all(bf16[16,48,128]{2,1,0:T(8,128)(2,1)S(1)} %physics.1), channel_id=1, replica_groups=mesh['lev'=16,'lat'=64] {'lev'}, dimensions={0} | all-to-all | bytes 393216 | tf_op jit(solution)/shard_map/all_to_all | solution.py:208
  53.2 0.8 %unpack.1 = f32[4,3,8,1024]{3,2,1,0:T(8,128)} custom-call(bf16[16,48,128]{2,1,0:T(8,128)(2,1)S(1)} %all_to_all.10.data_ref), custom_call_target="tpu_custom_call" | custom-call | tf_op jit(solution)/shard_map/unpack/pallas_call | solution.py:209
  (1 shorter events, 0.0 us)
Async XLA Ops:
  0.0 1.0 %copy-start.1 = (f32[4,8,3,1024]{3,1,2,0:T(8,128)S(1)}, f32[4,8,3,1024]{3,1,2,0:T(8,128)}, u32[]{:S(2)}) copy-start(f32[4,8,3,1024]{3,1,2,0:T(8,128)} %param.9) | copy-start | bytes 1179652
  1.0 0.9 %copy-start.4 = (f32[8,3,1024]{2,0,1:T(8,128)S(1)}, f32[8,3,1024]{2,0,1:T(8,128)}, u32[]{:S(2)}) copy-start(f32[8,3,1024]{2,0,1:T(8,128)} %param.11) | copy-start | bytes 294916
  1.9 32.8 %copy-start.2 = (bf16[512,1024]{1,0:T(8,128)(2,1)S(1)}, bf16[512,1024]{1,0:T(8,128)(2,1)}, u32[]{:S(2)}) copy-start(bf16[512,1024]{1,0:T(8,128)(2,1)} %w_in_ref.1) | copy-start | bytes 3145732
  1.9 7.8 %collective-permute-start = (bf16[5,8,1024]{2,1,0:T(8,128)(2,1)S(1)}, bf16[5,8,1024]{2,1,0:T(8,128)(2,1)S(1)}, u32[]{:S(2)}, u32[]{:S(2)}) collective-permute-start(bf16[5,8,1024]{2,1,0:T(8,128)(2,1)S(1)} %get-tuple-element.9), channel_id=1, source_target_pairs={{0,1},{1,2},{2,3},{3,4},{4,5},{5,6},{6,7},{7,8},{8,9},{9,10},{10,1... | collective-permute-start | bytes 245768 | tf_op jit(solution)/shard_map/ppermute | solution.py:178
  3.8 6.0 %collective-permute-start.1 = (bf16[4,8,1024]{2,1,0:T(8,128)(2,1)S(1)}, bf16[4,8,1024]{2,1,0:T(8,128)(2,1)S(1)}, u32[]{:S(2)}, u32[]{:S(2)}) collective-permute-start(bf16[4,8,1024]{2,1,0:T(8,128)(2,1)S(1)} %get-tuple-element.10), channel_id=1, source_target_pairs={{1,0},{2,1},{3,2},{4,3},{5,4},{6,5},{7,6},{8,7},{9,8},{10,9},{11,1... | collective-permute-start | bytes 196616 | tf_op jit(solution)/shard_map/ppermute | solution.py:179
  9.8 0.9 %copy-start.5 = (f32[8,3,1024]{2,0,1:T(8,128)S(1)}, f32[8,3,1024]{2,0,1:T(8,128)}, u32[]{:S(2)}) copy-start(f32[8,3,1024]{2,0,1:T(8,128)} %param.10) | copy-start | bytes 294916
  11.9 22.7 %all-to-all-start = ((bf16[16,48,128]{2,1,0:T(8,128)(2,1)}), bf16[16,48,128]{2,1,0:T(8,128)(2,1)S(1)}, u32[]{:S(2)}, u32[]{:S(2)}) async-start(bf16[16,48,128]{2,1,0:T(8,128)(2,1)} %flux.1), calls=%async_computation | async-start | bytes 393216 | tf_op jit(solution)/shard_map/all_to_all | solution.py:198
  25.7 0.8 %copy-start.6 = (f32[128,128]{1,0:T(8,128)S(1)}, f32[128,128]{1,0:T(8,128)}, u32[]{:S(2)}) copy-start(f32[128,128]{1,0:T(8,128)} %weight_ref.1) | copy-start | bytes 196612
  34.7 1.6 %copy-start = (bf16[1024,1024]{1,0:T(8,128)(2,1)S(1)}, bf16[1024,1024]{1,0:T(8,128)(2,1)}, u32[]{:S(2)}) copy-start(bf16[1024,1024]{1,0:T(8,128)(2,1)} %w_mid_ref.1) | copy-start | bytes 6291460
  36.3 1.2 %copy-start.3 = (bf16[1024,512]{1,0:T(8,128)(2,1)S(1)}, bf16[1024,512]{1,0:T(8,128)(2,1)}, u32[]{:S(2)}) copy-start(bf16[1024,512]{1,0:T(8,128)(2,1)} %w_out_ref.1) | copy-start | bytes 3145732
  37.5 0.7 %copy-start.7 = (s32[1,1,8]{2,1,0:T(1,128)S(1)}, s32[1,1,8]{2,1,0:T(1,128)}, u32[]{:S(2)}) copy-start(s32[1,1,8]{2,1,0:T(1,128)} %list_ref.1) | copy-start | bytes 100

commit v2 on v1

v2 whole, which is shorter than its diff:
```python
import jax
import jax.numpy as jnp
from jax import lax
from jax.experimental import pallas as pl
from jax.experimental.pallas import tpu as pltpu
from jax.sharding import PartitionSpec as P

NB = 8
F32 = jnp.float32
BF16 = jnp.bfloat16
VM = pltpu.VMEM


def whole():
    return pl.BlockSpec(memory_space=VM)


def in_hbm(array):
    return pltpu.with_memory_space_constraint(array, pltpu.HBM)


def cost(flops, moved):
    return pl.CostEstimate(flops=flops, bytes_accessed=moved, transcendentals=0)


def params(mib):
    return pltpu.CompilerParams(vmem_limit_bytes=mib * 2**20)


def load_kernel(state_ref, east_ref, north_ref, cells_ref, easterly_ref, northerly_ref, up_ref, down_ref, sems):
    fields, rows = state_ref.shape[:2]
    last = rows - 1

    def bring(source, target, k):
        copy = pltpu.make_async_copy(source, target, sems.at[k])
        copy.start()
        return copy

    first = [
        bring(state_ref.at[:, last], cells_ref.at[:, last], 0),
        bring(north_ref.at[last], northerly_ref.at[last], 1),
        bring(state_ref.at[:, 0], cells_ref.at[:, 0], 2),
    ]
    rest = [
        bring(state_ref.at[:, 1:last], cells_ref.at[:, 1:last], 3),
        bring(north_ref.at[:last], northerly_ref.at[:last], 4),
        bring(east_ref, easterly_ref, 5),
    ]
    for copy in first:
        copy.wait()
    for f in range(fields):
        up_ref[f] = cells_ref[f, last].astype(BF16)
        down_ref[f] = cells_ref[f, 0].astype(BF16)
    up_ref[fields] = northerly_ref[last].astype(BF16)
    for copy in rest:
        copy.wait()


def pair_remap(weight):
    n = weight.shape[0]
    row = lax.broadcasted_iota(jnp.int32, (n, n), 0)
    col = lax.broadcasted_iota(jnp.int32, (n, n), 1)
    raw = weight + jnp.where(row == col, 16.0, 0.0)
    remap = (raw / jnp.sum(raw, axis=1, keepdims=True)).T
    zero = jnp.zeros((8, n), F32)
    rows = []
    for m in range(n // 8):
        piece = remap[m * 8 : (m + 1) * 8]
        rows.append(jnp.concatenate([piece, zero], axis=1))
        rows.append(jnp.concatenate([zero, piece], axis=1))
    return jnp.concatenate(rows, axis=0)


def local_kernel(
    state_ref, east_ref, north_ref, list_ref, count_ref, weight_ref, w_in_ref, w_mid_ref,
    out_ref, high_ref, low_ref, mask_ref, w_in_out, w_mid_out, order, weight, sems,
):
    copies = [
        pltpu.make_async_copy(source, target, sems.at[k])
        for k, (source, target) in enumerate(
            ((list_ref, order), (weight_ref, weight), (w_in_ref, w_in_out), (w_mid_ref, w_mid_out))
        )
    ]
    for copy in copies:
        copy.start()
    fields, rows, _, width = state_ref.shape
    for f in range(fields):
        below_flux = None
        for j in range(rows):
            cells = state_ref[f, j]
            wind = north_ref[j]
            easterly = east_ref[j]
            east_cells = pltpu.roll(cells, width - 1, 1)
            east_flux = jnp.maximum(easterly, 0.0) * cells + jnp.minimum(easterly, 0.0) * east_cells
            west_flux = pltpu.roll(east_flux, 1, 1)
            value = cells - (east_flux - west_flux)
            if below_flux is not None:
                value = value + below_flux
            if j < rows - 1:
                below_flux = jnp.maximum(wind, 0.0) * cells + jnp.minimum(wind, 0.0) * state_ref[f, j + 1]
                value = value - below_flux
            out_ref[f, j] = value
    for copy in copies[:2]:
        copy.wait()
    pair = pair_remap(weight[...])
    high = pair.astype(BF16)
    high_ref[...] = high
    low_ref[...] = (pair - high.astype(F32)).astype(BF16)
    bits = jnp.int32(0)
    count = count_ref[0, 0]
    for s in range(NB):
        bits = bits + jnp.where(s < count, jnp.left_shift(jnp.int32(1), order[0, 0, s]), 0)
    odd = lax.rem(lax.axis_index("lev"), 2)
    place = lax.broadcasted_iota(jnp.int32, mask_ref.shape, 0)
    column = jnp.where(place < 128, place + 64 * odd, place - 128 * odd)
    block = jnp.right_shift(column * 2731, 16)
    active = jnp.bitwise_and(jnp.right_shift(jnp.full(mask_ref.shape, bits), block), 1)
    mask_ref[...] = active.astype(F32)
    for copy in copies[2:]:
        copy.wait()


def finish_kernel(local_ref, state_ref, north_ref, south_edge_ref, north_edge_ref, out_ref):
    fields, rows = state_ref.shape[:2]
    last = rows - 1
    wall = lax.axis_index("lat") == lax.axis_size("lat") - 1
    wind = north_ref[last] * jnp.where(wall, 0.0, 1.0).astype(F32)
    wind_below = south_edge_ref[fields].astype(F32)
    rising, sinking = jnp.maximum(wind, 0.0), jnp.minimum(wind, 0.0)
    rising_below, sinking_below = jnp.maximum(wind_below, 0.0), jnp.minimum(wind_below, 0.0)
    low = lax.broadcasted_iota(jnp.int32, (8, 128), 1) < 64
    updated = []
    for f in range(fields):
        south = rising_below * south_edge_ref[f].astype(F32) + sinking_below * state_ref[f, 0]
        north = rising * state_ref[f, last] + sinking * north_edge_ref[f].astype(F32)
        pieces = [local_ref[f, j] for j in range(rows)]
        pieces[0] = pieces[0] + south
        pieces[last] = pieces[last] - north
        updated.append(pieces)

    def tile(f, v):
        j, k = divmod(v, 8)
        return updated[f][j][:, k * 128 : (k + 1) * 128]

    for p in range(8):
        full_a = [tile(f, 3 * p) for f in range(fields)]
        half = [tile(f, 3 * p + 1) for f in range(fields)]
        full_b = [tile(f, 3 * p + 2) for f in range(fields)]
        turned = [pltpu.roll(h, 64, 1) for h in half]
        half_a = [jnp.where(low, half[f], turned[f + 2]) for f in range(2)]
        half_b = [jnp.where(low, turned[f], half[f + 2]) for f in range(2)]
        out_ref[2 * p] = jnp.concatenate(full_a + half_a, axis=0).astype(BF16)
        out_ref[2 * p + 1] = jnp.concatenate(full_b + half_b, axis=0).astype(BF16)


def silu(v):
    return v / (1.0 + jnp.exp(-v))


def physics_kernel(
    data_ref, high_ref, low_ref, mask_ref, w_in_ref, w_mid_ref, w_out_ref, out_ref, w_out, sem
):
    last_layer = pltpu.make_async_copy(w_out_ref, w_out, sem)
    last_layer.start()

    def turned(r):
        block = data_ref[:, r : r + 16, :].reshape(256, 128)
        return block.T

    ends = turned(32)
    x = []
    for p in range(2):
        cols = jnp.concatenate([turned(16 * p), ends[64 * p : 64 * p + 64]], axis=0)
        x.append(
            jnp.dot(cols, high_ref[...], preferred_element_type=F32)
            + jnp.dot(cols, low_ref[...], preferred_element_type=F32)
        )
    remapped = jnp.concatenate(x, axis=1)
    first = silu(jnp.dot(remapped.astype(BF16), w_in_ref[...], preferred_element_type=F32)).astype(BF16)
    second = silu(jnp.dot(first, w_mid_ref[...], preferred_element_type=F32)).astype(BF16)
    last_layer.wait()
    tendency = jnp.dot(second, w_out[...], preferred_element_type=F32)
    active = jnp.concatenate([mask_ref[...]] * 4, axis=1) > 0.0
    finished = remapped + jnp.where(active, tendency, 0.0)

    def put(r, rows):
        back = rows.T.reshape(2, 16, 8, 128)
        both = jnp.concatenate([back[0], back[1]], axis=1)
        out_ref[:, r : r + 16, :] = both.astype(BF16)

    put(0, finished[:128, :256])
    put(16, finished[:128, 256:])
    put(32, jnp.concatenate([finished[128:, :256], finished[128:, 256:]], axis=0))


def unpack_kernel(data_ref, out_ref):
    fields = out_ref.shape[0]
    lane = lax.broadcasted_iota(jnp.int32, (16, 128), 1)
    low = lane < 64

    def put(v, pair, value):
        j, k = divmod(v, 8)
        for f in range(2):
            out_ref[2 * pair + f, j, :, k * 128 : (k + 1) * 128] = value[8 * f : 8 * f + 8]

    for p in range(8):
        a = data_ref[2 * p].astype(F32)
        b = data_ref[2 * p + 1].astype(F32)
        for pair in range(2):
            put(3 * p, pair, a[16 * pair : 16 * pair + 16])
            put(3 * p + 2, pair, b[16 * pair : 16 * pair + 16])
        end_a, end_b = a[32:], b[32:]
        put(3 * p + 1, 0, jnp.where(low, end_a, pltpu.roll(end_b, 64, 1)))
        put(3 * p + 1, 1, jnp.where(low, pltpu.roll(end_a, 64, 1), end_b))


def per_device(
    state, wind_east, wind_north, remap_weight, block_list, block_count, w_in, w_mid, w_out
):
    fields, lev_dev, lat_rows, lon_cells = state.shape
    lev_count = lax.axis_size("lev")
    lat_count = lax.axis_size("lat")
    cells = jnp.transpose(state, (0, 2, 1, 3))
    east = jnp.transpose(wind_east, (1, 0, 2))
    north = jnp.transpose(wind_north, (1, 0, 2))
    edge = (lev_dev, lon_cells)
    smem = pl.BlockSpec(memory_space=pltpu.SMEM)
    hbm = pl.BlockSpec(memory_space=pltpu.HBM)
    levels = lev_dev * lev_count
    col_count = lat_rows * lon_cells // lev_count
    held_cells, held_east, held_north, up, down = pl.pallas_call(
        load_kernel,
        out_shape=[
            jax.ShapeDtypeStruct(cells.shape, F32),
            jax.ShapeDtypeStruct(east.shape, F32),
            jax.ShapeDtypeStruct(north.shape, F32),
            jax.ShapeDtypeStruct((fields + 1, *edge), BF16),
            jax.ShapeDtypeStruct((fields, *edge), BF16),
        ],
        in_specs=[hbm] * 3,
        out_specs=[whole()] * 5,
        scratch_shapes=[pltpu.SemaphoreType.DMA((6,))],
        compiler_params=params(4),
        cost_estimate=cost(1 << 17, 1 << 21),
        name="load",
    )(*map(in_hbm, (cells, east, north)))
    south_edge = lax.ppermute(up, "lat", [(i, i + 1) for i in range(lat_count - 1)])
    north_edge = lax.ppermute(down, "lat", [(i + 1, i) for i in range(lat_count - 1)])
    local, high, low, mask, held_in, held_mid = pl.pallas_call(
        local_kernel,
        out_shape=[
            jax.ShapeDtypeStruct(cells.shape, F32),
            jax.ShapeDtypeStruct((2 * levels, 2 * levels), BF16),
            jax.ShapeDtypeStruct((2 * levels, 2 * levels), BF16),
            jax.ShapeDtypeStruct((col_count, 128), F32),
            jax.ShapeDtypeStruct(w_in.shape, BF16),
            jax.ShapeDtypeStruct(w_mid.shape, BF16),
        ],
        in_specs=[whole()] * 3 + [hbm, smem] + [hbm] * 3,
        out_specs=[whole()] * 6,
        scratch_shapes=[
            pltpu.SMEM(block_list.shape, jnp.int32),
            VM(remap_weight.shape, F32),
            pltpu.SemaphoreType.DMA((4,)),
        ],
        compiler_params=params(4),
        cost_estimate=cost(1 << 22, 1 << 22),
        name="local",
    )(held_cells, held_east, held_north, in_hbm(block_list), block_count, *map(in_hbm, (remap_weight, w_in, w_mid)))
    chunk = (lev_count, fields * lev_dev * lat_rows * lon_cells // lev_count // 128, 128)
    packed = pl.pallas_call(
        finish_kernel,
        out_shape=jax.ShapeDtypeStruct(chunk, BF16),
        in_specs=[whole()] * 5,
        out_specs=whole(),
        compiler_params=params(4),
        cost_estimate=cost(1 << 20, 1 << 20),
        name="finish",
    )(local, held_cells, held_north, south_edge, north_edge)
    packed, high, low, mask, held_in, held_mid = lax.optimization_barrier(
        (packed, high, low, mask, held_in, held_mid)
    )
    columns = lax.all_to_all(packed, "lev", split_axis=0, concat_axis=0, tiled=True)
    finished = pl.pallas_call(
        physics_kernel,
        out_shape=jax.ShapeDtypeStruct(chunk, BF16),
        in_specs=[whole()] * 6 + [hbm],
        out_specs=whole(),
        scratch_shapes=[VM(w_out.shape, BF16), pltpu.SemaphoreType.DMA(())],
        compiler_params=params(16),
        cost_estimate=cost(1 << 30, 1 << 22),
        name="physics",
    )(columns, high, low, mask, held_in, held_mid, in_hbm(w_out))
    returned = lax.all_to_all(finished, "lev", split_axis=0, concat_axis=0, tiled=True)
    result = pl.pallas_call(
        unpack_kernel,
        out_shape=jax.ShapeDtypeStruct(cells.shape, F32),
        in_specs=[whole()],
        out_specs=whole(),
        compiler_params=params(4),
        cost_estimate=cost(1 << 18, 1 << 20),
        name="unpack",
    )(returned)
    return jnp.transpose(result, (0, 2, 1, 3))


def solution(mesh):
    placed = (
        P(None, "lev", "lat", None),
        P("lev", "lat", None),
        P("lev", "lat", None),
        P(),
        P("lev", "lat", None),
        P("lev", "lat"),
        P(),
        P(),
        P(),
    )
    return jax.shard_map(
        per_device,
        mesh=mesh,
        in_specs=placed,
        out_specs=P(None, "lev", "lat", None),
        check_vma=False,
    )
```

time: 54.5 us -> 49.9 us (0.916)
  blocking collectives: 13.1 us -> 37.1 us
  starting transfers between devices: 16.3 us -> 3.04 us
  waiting for transfers between devices: 12.6 us -> 1.57 us
  local copies, waits for them, and re-layouts: 7.09 us -> 0 us
  Pallas kernels: 4.23 us -> 7.14 us
    all_to_all x0 -> x1, blocking collectives: none -> 23.3 us  [per_device(): lax.all_to_all(packed, 'lev', split_axis=0, concat_axis=0, tiled=True)]
    all_to_all x1 -> x0, starting transfers between devices: 13.1 us -> none  [per_device(): lax.all_to_all(packed, 'lev', split_axis=0, concat_axis=0, tiled=True)]
    all_to_all x1 -> x0, waiting for transfers between devices: 7.92 us -> none  [per_device(): lax.all_to_all(packed, 'lev', split_axis=0, concat_axis=0, tiled=True)]
    unnamed x16 -> x0, local copies, waits for them, and re-layouts: 7.09 us -> none
    ppermute x1, waiting for transfers between devices: 4.65 us -> 1.56 us  [per_device(): lax.ppermute(down, 'lat', [(i + 1, i) for i in range(lat_count - 1)])]
    pallas_call x3, Pallas kernels: 1.48 us -> 3.76 us  [the longest x1 2.44 us: per_device(): pl.pallas_call(local_kernel, out_shape=[jax.ShapeDtypeStruct(cells.shape,...]
    all_to_all x1, blocking collectives: 13.1 us -> 13.8 us  [per_device(): lax.all_to_all(finished, 'lev', split_axis=0, concat_axis=0, tiled=True)]
    pallas_call x1, Pallas kernels: 1.91 us -> 2.55 us  [per_device(): pl.pallas_call(physics_kernel, out_shape=jax.ShapeDtypeStruct(chunk, BF16...]
  transfers between devices with their start and end apart: 3 -> 2, of which waited for: 2 -> 1; matrix products, arithmetic and copies ran while one was open for 0% -> 0% of each run, Pallas kernels for 0% -> 5%
where the time goes in v2:
time: 49.9 us; the launch traced here: 49.6 us
  blocking collectives  37.1 us (74%)
  Pallas kernels  7.14 us (14%)
  starting transfers between devices  3.04 us (6%)
  waiting for transfers between devices  1.57 us (3%)
  between operations  0.69 us (1%)
    all_to_all x1, blocking collectives, per_device(): lax.all_to_all(packed, 'lev', split_axis=0, concat_axis=0, tiled=True)  23.3 us
    all_to_all x1, blocking collectives, per_device(): lax.all_to_all(finished, 'lev', split_axis=0, concat_axis=0, tiled=True)  13.8 us
    pallas_call x1, Pallas kernels, per_device(): pl.pallas_call(physics_kernel, out_shape=jax.ShapeDtypeStruct(chunk, BF16...  2.55 us
    pallas_call x1, Pallas kernels, per_device(): pl.pallas_call(local_kernel, out_shape=[jax.ShapeDtypeStruct(cells.shape,...  2.44 us
    ppermute x1, starting transfers between devices, per_device(): lax.ppermute(up, 'lat', [(i, i + 1) for i in range(lat_count - 1)])  1.74 us
    ppermute x1, waiting for transfers between devices, per_device(): lax.ppermute(down, 'lat', [(i + 1, i) for i in range(lat_count - 1)])  1.56 us
    ppermute x1, starting transfers between devices, per_device(): lax.ppermute(down, 'lat', [(i + 1, i) for i in range(lat_count - 1)])  1.29 us
    pallas_call x1, Pallas kernels, per_device(): pl.pallas_call(load_kernel, out_shape=[jax.ShapeDtypeStruct(cells.shape,...  1.19 us
  transfers between devices with their start and end apart: 2, of which 1 were waited for; matrix products, arithmetic and copies ran while one was open for 0% of the time, Pallas kernels for 5%

profile of v2, /device:TPU:8, one launch (start us, length us, event | category | flops | bytes accessed | tf_op | source)
XLA Modules:
  0.0 49.6 jit_solution(5271083468371847279)
XLA Ops:
  0.0 1.2 %load.1 = (f32[4,3,8,1024]{3,2,1,0:T(8,128)S(1)}, f32[3,8,1024]{2,1,0:T(8,128)S(1)}, f32[3,8,1024]{2,1,0:T(8,128)S(1)}, bf16[5,8,1024]{2,1,0:T(8,128)(2,1)S(1)}, bf16[4,8,1024]{2,1,0:T(8,128)(2,1)S(1)}) custom-call(f32[4,3,8,1024]{3,2,1,0:T(8,128)} %bitcast.4, f32[3,8,1024]{2,1,0:T(8,128)} %bitcast.5, f32[3,8,1024]{2,1,0:T(8,128)} %bitcast.6), custom_call_target="tpu_custom_call" | custom-call | flops 131072 | bytes 2097152 | tf_op jit(solution)/shard_map/load/pallas_call | solution.py:231
  1.2 1.7 %collective-permute-start = (bf16[5,8,1024]{2,1,0:T(8,128)(2,1)S(1)}, bf16[5,8,1024]{2,1,0:T(8,128)(2,1)S(1)}, u32[]{:S(2)}, u32[]{:S(2)}) collective-permute-start(bf16[5,8,1024]{2,1,0:T(8,128)(2,1)S(1)} %get-tuple-element.26), channel_id=1, source_target_pairs={{0,1},{1,2},{2,3},{3,4},{4,5},{5,6},{6,7},{7,8},{8,9},{9,10},{10,1... | collective-permute-start | bytes 245768 | tf_op jit(solution)/shard_map/ppermute | solution.py:247
  2.9 1.3 %collective-permute-start.1 = (bf16[4,8,1024]{2,1,0:T(8,128)(2,1)S(1)}, bf16[4,8,1024]{2,1,0:T(8,128)(2,1)S(1)}, u32[]{:S(2)}, u32[]{:S(2)}) collective-permute-start(bf16[4,8,1024]{2,1,0:T(8,128)(2,1)S(1)} %get-tuple-element.27), channel_id=1, source_target_pairs={{1,0},{2,1},{3,2},{4,3},{5,4},{6,5},{7,6},{8,7},{9,8},{10,9},{11,1... | collective-permute-start | bytes 196616 | tf_op jit(solution)/shard_map/ppermute | solution.py:248
  4.9 2.4 %local.1 = (f32[4,3,8,1024]{3,2,1,0:T(8,128)S(1)}, bf16[256,256]{1,0:T(8,128)(2,1)S(1)}, bf16[256,256]{1,0:T(8,128)(2,1)S(1)}, f32[192,128]{1,0:T(8,128)S(1)}, b...) custom-call(f32[4,3,8,1024]{3,2,1,0:T(8,128)S(1)} %get-tuple-element.22.state_ref, ...), custom_call_target="tpu_custom_call" | custom-call | flops 4194304 | bytes 4194304 | tf_op jit(solution)/shard_map/local/pallas_call | solution.py:249
  7.3 1.6 %collective-permute-done.1.north_edge_ref = bf16[4,8,1024]{2,1,0:T(8,128)(2,1)S(1)} collective-permute-done((bf16[4,8,1024]{2,1,0:T(8,128)(2,1)S(1)}, bf16[4,8,1024]{2,1,0:T(8,128)(2,1)S(1)}, u32[]{:S(2)}, u32[]{:S(2)}) %collective-permute-start.1) | collective-permute-done | bytes 65568 | tf_op jit(solution)/shard_map/ppermute | solution.py:248
  8.9 0.0 collective-permute-done.south_edge_ref
  8.9 0.1 finish.1
  9.0 23.3 %all_to_all.10.data_ref = bf16[16,48,128]{2,1,0:T(8,128)(2,1)S(1)} all-to-all(bf16[16,48,128]{2,1,0:T(8,128)(2,1)S(1)} %finish.1), channel_id=1, replica_groups=mesh['lev'=16,'lat'=64] {'lev'}, dimensions={0} | all-to-all | bytes 393216 | tf_op jit(solution)/shard_map/all_to_all | solution.py:283
  32.4 2.6 %physics.1 = bf16[16,48,128]{2,1,0:T(8,128)(2,1)S(1)} custom-call(bf16[16,48,128]{2,1,0:T(8,128)(2,1)S(1)} %all_to_all.10.data_ref, bf16[256,256]{1,0:T(8,128)(2,1)S(1)} %get-tuple-element.34.high_ref, bf16[256,256]{1,0:T(8,128)(2,1)S(1)} %get-tuple-element.35.low_ref, f32[192,128]{1,0:T(8,128)S(1)} %get-tuple-element.36.mask_ref, ...), custom_call_target="tpu_custom_call" | custom-call | flops 1073741824 | bytes 4194304 | tf_op jit(solution)/shard_map/physics/pallas_call | solution.py:284
  34.9 13.8 %all_to_all.11.data_ref = bf16[16,48,128]{2,1,0:T(8,128)(2,1)S(1)} all-to-all(bf16[16,48,128]{2,1,0:T(8,128)(2,1)S(1)} %physics.1), channel_id=1, replica_groups=mesh['lev'=16,'lat'=64] {'lev'}, dimensions={0} | all-to-all | bytes 393216 | tf_op jit(solution)/shard_map/all_to_all | solution.py:294
  48.7 0.8 %unpack.1 = f32[4,3,8,1024]{3,2,1,0:T(8,128)} custom-call(bf16[16,48,128]{2,1,0:T(8,128)(2,1)S(1)} %all_to_all.11.data_ref), custom_call_target="tpu_custom_call" | custom-call | flops 262144 | bytes 1048576 | tf_op jit(solution)/shard_map/unpack/pallas_call | solution.py:295
Async XLA Ops:
  1.2 7.7 %collective-permute-start = (bf16[5,8,1024]{2,1,0:T(8,128)(2,1)S(1)}, bf16[5,8,1024]{2,1,0:T(8,128)(2,1)S(1)}, u32[]{:S(2)}, u32[]{:S(2)}) collective-permute-start(bf16[5,8,1024]{2,1,0:T(8,128)(2,1)S(1)} %get-tuple-element.26), channel_id=1, source_target_pairs={{0,1},{1,2},{2,3},{3,4},{4,5},{5,6},{6,7},{7,8},{8,9},{9,10},{10,1... | collective-permute-start | bytes 245768 | tf_op jit(solution)/shard_map/ppermute | solution.py:247
  2.9 6.0 %collective-permute-start.1 = (bf16[4,8,1024]{2,1,0:T(8,128)(2,1)S(1)}, bf16[4,8,1024]{2,1,0:T(8,128)(2,1)S(1)}, u32[]{:S(2)}, u32[]{:S(2)}) collective-permute-start(bf16[4,8,1024]{2,1,0:T(8,128)(2,1)S(1)} %get-tuple-element.27), channel_id=1, source_target_pairs={{1,0},{2,1},{3,2},{4,3},{5,4},{6,5},{7,6},{8,7},{9,8},{10,9},{11,1... | collective-permute-start | bytes 196616 | tf_op jit(solution)/shard_map/ppermute | solution.py:248

commit v3 on v2

--- a/solution.py
+++ b/solution.py
@@ -27,7 +27,11 @@
     return pltpu.CompilerParams(vmem_limit_bytes=mib * 2**20)
 
 
-def load_kernel(state_ref, east_ref, north_ref, cells_ref, easterly_ref, northerly_ref, up_ref, down_ref, sems):
+def even_band():
+    return lax.rem(lax.axis_index("lat"), 2) == 0
+
+
+def load_kernel(state_ref, east_ref, north_ref, cells_ref, easterly_ref, northerly_ref, near_ref, far_ref, sems):
     fields, rows = state_ref.shape[:2]
     last = rows - 1
 
@@ -40,18 +44,19 @@
         bring(state_ref.at[:, last], cells_ref.at[:, last], 0),
         bring(north_ref.at[last], northerly_ref.at[last], 1),
         bring(state_ref.at[:, 0], cells_ref.at[:, 0], 2),
+        bring(north_ref.at[:last], northerly_ref.at[:last], 4),
     ]
     rest = [
         bring(state_ref.at[:, 1:last], cells_ref.at[:, 1:last], 3),
-        bring(north_ref.at[:last], northerly_ref.at[:last], 4),
         bring(east_ref, easterly_ref, 5),
     ]
     for copy in first:
         copy.wait()
-    for f in range(fields):
-        up_ref[f] = cells_ref[f, last].astype(BF16)
-        down_ref[f] = cells_ref[f, 0].astype(BF16)
-    up_ref[fields] = northerly_ref[last].astype(BF16)
+    near_row = jnp.where(even_band(), last, 0)
+    for edge_ref, row in ((near_ref, near_row), (far_ref, last - near_row)):
+        for f in range(fields):
+            edge_ref[f] = cells_ref[f, row].astype(BF16)
+        edge_ref[fields] = northerly_ref[row].astype(BF16)
     for copy in rest:
         copy.wait()
 
@@ -72,13 +77,13 @@
 
 
 def local_kernel(
-    state_ref, east_ref, north_ref, list_ref, count_ref, weight_ref, w_in_ref, w_mid_ref,
-    out_ref, high_ref, low_ref, mask_ref, w_in_out, w_mid_out, order, weight, sems,
+    state_ref, east_ref, north_ref, list_ref, count_ref, weight_ref,
+    out_ref, high_ref, low_ref, mask_ref, order, weight, sems,
 ):
     copies = [
         pltpu.make_async_copy(source, target, sems.at[k])
         for k, (source, target) in enumerate(
-            ((list_ref, order), (weight_ref, weight), (w_in_ref, w_in_out), (w_mid_ref, w_mid_out))
+            ((list_ref, order), (weight_ref, weight))
         )
     ]
     for copy in copies:
@@ -100,7 +105,7 @@
                 below_flux = jnp.maximum(wind, 0.0) * cells + jnp.minimum(wind, 0.0) * state_ref[f, j + 1]
                 value = value - below_flux
             out_ref[f, j] = value
-    for copy in copies[:2]:
+    for copy in copies:
         copy.wait()
     pair = pair_remap(weight[...])
     high = pair.astype(BF16)
@@ -116,23 +121,26 @@
     block = jnp.right_shift(column * 2731, 16)
     active = jnp.bitwise_and(jnp.right_shift(jnp.full(mask_ref.shape, bits), block), 1)
     mask_ref[...] = active.astype(F32)
-    for copy in copies[2:]:
-        copy.wait()
-
-
-def finish_kernel(local_ref, state_ref, north_ref, south_edge_ref, north_edge_ref, out_ref):
+
+
+def finish_kernel(local_ref, state_ref, north_ref, near_ref, far_ref, out_ref):
     fields, rows = state_ref.shape[:2]
     last = rows - 1
     wall = lax.axis_index("lat") == lax.axis_size("lat") - 1
     wind = north_ref[last] * jnp.where(wall, 0.0, 1.0).astype(F32)
-    wind_below = south_edge_ref[fields].astype(F32)
+    even = even_band()
+
+    def edge(first, second, f):
+        return jnp.where(even, first[f].astype(F32), second[f].astype(F32))
+
+    wind_below = edge(far_ref, near_ref, fields)
     rising, sinking = jnp.maximum(wind, 0.0), jnp.minimum(wind, 0.0)
     rising_below, sinking_below = jnp.maximum(wind_below, 0.0), jnp.minimum(wind_below, 0.0)
     low = lax.broadcasted_iota(jnp.int32, (8, 128), 1) < 64
     updated = []
     for f in range(fields):
-        south = rising_below * south_edge_ref[f].astype(F32) + sinking_below * state_ref[f, 0]
-        north = rising * state_ref[f, last] + sinking * north_edge_ref[f].astype(F32)
+        south = rising_below * edge(far_ref, near_ref, f) + sinking_below * state_ref[f, 0]
+        north = rising * state_ref[f, last] + sinking * edge(near_ref, far_ref, f)
         pieces = [local_ref[f, j] for j in range(rows)]
         pieces[0] = pieces[0] + south
         pieces[last] = pieces[last] - north
@@ -158,11 +166,8 @@
 
 
 def physics_kernel(
-    data_ref, high_ref, low_ref, mask_ref, w_in_ref, w_mid_ref, w_out_ref, out_ref, w_out, sem
+    data_ref, high_ref, low_ref, mask_ref, w_in_ref, w_mid_ref, w_out_ref, out_ref
 ):
-    last_layer = pltpu.make_async_copy(w_out_ref, w_out, sem)
-    last_layer.start()
-
     def turned(r):
         block = data_ref[:, r : r + 16, :].reshape(256, 128)
         return block.T
@@ -178,8 +183,7 @@
     remapped = jnp.concatenate(x, axis=1)
     first = silu(jnp.dot(remapped.astype(BF16), w_in_ref[...], preferred_element_type=F32)).astype(BF16)
     second = silu(jnp.dot(first, w_mid_ref[...], preferred_element_type=F32)).astype(BF16)
-    last_layer.wait()
-    tendency = jnp.dot(second, w_out[...], preferred_element_type=F32)
+    tendency = jnp.dot(second, w_out_ref[...], preferred_element_type=F32)
     active = jnp.concatenate([mask_ref[...]] * 4, axis=1) > 0.0
     finished = remapped + jnp.where(active, tendency, 0.0)
 
@@ -212,6 +216,11 @@
         end_a, end_b = a[32:], b[32:]
         put(3 * p + 1, 0, jnp.where(low, end_a, pltpu.roll(end_b, 64, 1)))
         put(3 * p + 1, 1, jnp.where(low, pltpu.roll(end_a, 64, 1), end_b))
+
+
+def pairs(start, count):
+    lower = range(start, count - 1, 2)
+    return [(i, i + 1) for i in lower] + [(i + 1, i) for i in lower]
 
 
 def per_device(
@@ -228,14 +237,14 @@
     hbm = pl.BlockSpec(memory_space=pltpu.HBM)
     levels = lev_dev * lev_count
     col_count = lat_rows * lon_cells // lev_count
-    held_cells, held_east, held_north, up, down = pl.pallas_call(
+    held_cells, held_east, held_north, near, far = pl.pallas_call(
         load_kernel,
         out_shape=[
             jax.ShapeDtypeStruct(cells.shape, F32),
             jax.ShapeDtypeStruct(east.shape, F32),
             jax.ShapeDtypeStruct(north.shape, F32),
             jax.ShapeDtypeStruct((fields + 1, *edge), BF16),
-            jax.ShapeDtypeStruct((fields, *edge), BF16),
+            jax.ShapeDtypeStruct((fields + 1, *edge), BF16),
         ],
         in_specs=[hbm] * 3,
         out_specs=[whole()] * 5,
@@ -244,29 +253,27 @@
         cost_estimate=cost(1 << 17, 1 << 21),
         name="load",
     )(*map(in_hbm, (cells, east, north)))
-    south_edge = lax.ppermute(up, "lat", [(i, i + 1) for i in range(lat_count - 1)])
-    north_edge = lax.ppermute(down, "lat", [(i + 1, i) for i in range(lat_count - 1)])
-    local, high, low, mask, held_in, held_mid = pl.pallas_call(
+    far = lax.ppermute(far, "lat", pairs(1, lat_count))
+    near = lax.ppermute(near, "lat", pairs(0, lat_count))
+    local, high, low, mask = pl.pallas_call(
         local_kernel,
         out_shape=[
             jax.ShapeDtypeStruct(cells.shape, F32),
             jax.ShapeDtypeStruct((2 * levels, 2 * levels), BF16),
             jax.ShapeDtypeStruct((2 * levels, 2 * levels), BF16),
             jax.ShapeDtypeStruct((col_count, 128), F32),
-            jax.ShapeDtypeStruct(w_in.shape, BF16),
-            jax.ShapeDtypeStruct(w_mid.shape, BF16),
         ],
-        in_specs=[whole()] * 3 + [hbm, smem] + [hbm] * 3,
-        out_specs=[whole()] * 6,
+        in_specs=[whole()] * 3 + [hbm, smem, hbm],
+        out_specs=[whole()] * 4,
         scratch_shapes=[
             pltpu.SMEM(block_list.shape, jnp.int32),
             VM(remap_weight.shape, F32),
-            pltpu.SemaphoreType.DMA((4,)),
+            pltpu.SemaphoreType.DMA((2,)),
         ],
         compiler_params=params(4),
         cost_estimate=cost(1 << 22, 1 << 22),
         name="local",
-    )(held_cells, held_east, held_north, in_hbm(block_list), block_count, *map(in_hbm, (remap_weight, w_in, w_mid)))
+    )(held_cells, held_east, held_north, in_hbm(block_list), block_count, in_hbm(remap_weight))
     chunk = (lev_count, fields * lev_dev * lat_rows * lon_cells // lev_count // 128, 128)
     packed = pl.pallas_call(
         finish_kernel,
@@ -274,23 +281,20 @@
         in_specs=[whole()] * 5,
         out_specs=whole(),
         compiler_params=params(4),
-        cost_estimate=cost(1 << 20, 1 << 20),
+        cost_estimate=cost(1 << 34, 1 << 20),
         name="finish",
-    )(local, held_cells, held_north, south_edge, north_edge)
-    packed, high, low, mask, held_in, held_mid = lax.optimization_barrier(
-        (packed, high, low, mask, held_in, held_mid)
-    )
+    )(local, held_cells, held_north, near, far)
+    packed, high, low, mask = lax.optimization_barrier((packed, high, low, mask))
     columns = lax.all_to_all(packed, "lev", split_axis=0, concat_axis=0, tiled=True)
     finished = pl.pallas_call(
         physics_kernel,
         out_shape=jax.ShapeDtypeStruct(chunk, BF16),
-        in_specs=[whole()] * 6 + [hbm],
+        in_specs=[whole()] * 7,
         out_specs=whole(),
-        scratch_shapes=[VM(w_out.shape, BF16), pltpu.SemaphoreType.DMA(())],
         compiler_params=params(16),
         cost_estimate=cost(1 << 30, 1 << 22),
         name="physics",
-    )(columns, high, low, mask, held_in, held_mid, in_hbm(w_out))
+    )(columns, high, low, mask, w_in, w_mid, w_out)
     returned = lax.all_to_all(finished, "lev", split_axis=0, concat_axis=0, tiled=True)
     result = pl.pallas_call(
         unpack_kernel,

time: 49.9 us -> 48.7 us (0.976)
  the two profiles are of different devices: /device:TPU:8 before, /device:TPU:1 now
where the time goes in v3:
time: 48.7 us; the launch traced here: 48.5 us
  blocking collectives  21.5 us (44%)
  starting transfers between devices  17.9 us (37%)
  Pallas kernels  5.02 us (10%)
  waiting for transfers between devices  3.31 us (7%)
  between operations  0.7 us (1%)
    ppermute x1, starting transfers between devices, per_device(): near = lax.ppermute(near, 'lat', pairs(0, lat_count))  16 us
    all_to_all x1, blocking collectives, per_device(): lax.all_to_all(finished, 'lev', split_axis=0, concat_axis=0, tiled=True)  11.2 us
    all_to_all x1, blocking collectives, per_device(): lax.all_to_all(packed, 'lev', split_axis=0, concat_axis=0, tiled=True)  10.3 us
    ppermute x1, waiting for transfers between devices, per_device(): far = lax.ppermute(far, 'lat', pairs(1, lat_count))  3.3 us
    ppermute x1, starting transfers between devices, per_device(): far = lax.ppermute(far, 'lat', pairs(1, lat_count))  1.92 us
    pallas_call x1, Pallas kernels, per_device(): pl.pallas_call(local_kernel, out_shape=[jax.ShapeDtypeStruct(cells.shape,...  1.5 us
    pallas_call x1, Pallas kernels, per_device(): pl.pallas_call(physics_kernel, out_shape=jax.ShapeDtypeStruct(chunk, BF16...  1.35 us
    pallas_call x1, Pallas kernels, per_device(): pl.pallas_call(load_kernel, out_shape=[jax.ShapeDtypeStruct(cells.shape,...  1.19 us
  transfers between devices with their start and end apart: 2, of which 1 were waited for; matrix products, arithmetic and copies ran while one was open for 0% of the time, Pallas kernels for 3%

profile of v3, /device:TPU:1, one launch (start us, length us, event | category | flops | bytes accessed | tf_op | source)
XLA Modules:
  0.0 48.5 jit_solution(15096608368930952334)
XLA Ops:
  0.0 1.2 %load.1 = (f32[4,3,8,1024]{3,2,1,0:T(8,128)S(1)}, f32[3,8,1024]{2,1,0:T(8,128)S(1)}, f32[3,8,1024]{2,1,0:T(8,128)S(1)}, bf16[5,8,1024]{2,1,0:T(8,128)(2,1)S(1)}, bf16[5,8,1024]{2,1,0:T(8,128)(2,1)S(1)}) custom-call(f32[4,3,8,1024]{3,2,1,0:T(8,128)} %bitcast.4, f32[3,8,1024]{2,1,0:T(8,128)} %bitcast.5, f32[3,8,1024]{2,1,0:T(8,128)} %bitcast.6), custom_call_target="tpu_custom_call" | custom-call | flops 131072 | bytes 2097152 | tf_op jit(solution)/shard_map/load/pallas_call | solution.py:240
  1.2 16.0 %collective-permute-start = (bf16[5,8,1024]{2,1,0:T(8,128)(2,1)S(1)}, bf16[5,8,1024]{2,1,0:T(8,128)(2,1)S(1)}, u32[]{:S(2)}, u32[]{:S(2)}) collective-permute-start(bf16[5,8,1024]{2,1,0:T(8,128)(2,1)S(1)} %get-tuple-element.22), channel_id=1, source_target_pairs={{0,1},{2,3},{4,5},{6,7},{8,9},{10,11},{12,13},{14,15},{16,17},{18,... | collective-permute-start | bytes 245768 | tf_op jit(solution)/shard_map/ppermute | solution.py:257
  17.2 1.9 %collective-permute-start.1 = (bf16[5,8,1024]{2,1,0:T(8,128)(2,1)S(1)}, bf16[5,8,1024]{2,1,0:T(8,128)(2,1)S(1)}, u32[]{:S(2)}, u32[]{:S(2)}) collective-permute-start(bf16[5,8,1024]{2,1,0:T(8,128)(2,1)S(1)} %get-tuple-element.23), channel_id=1, source_target_pairs={{1,2},{3,4},{5,6},{7,8},{9,10},{11,12},{13,14},{15,16},{17,18},{19... | collective-permute-start | bytes 245768 | tf_op jit(solution)/shard_map/ppermute | solution.py:256
  19.8 1.5 %local.1 = (f32[4,3,8,1024]{3,2,1,0:T(8,128)S(1)}, bf16[256,256]{1,0:T(8,128)(2,1)S(1)}, bf16[256,256]{1,0:T(8,128)(2,1)S(1)}, f32[192,128]{1,0:T(8,128)S(1)}) custom-call(f32[4,3,8,1024]{3,2,1,0:T(8,128)S(1)} %get-tuple-element.18.state_ref, f32[3,8,1024]{2,1,0:T(8,128)S(1)} %get-tuple-element.19.east_ref, f32[3,8,1024]{2,1,0:T(8,128)S(1)} %get-tuple-element.20.north_ref, ...), custom_call_target="tpu_custom_call" | custom-call | flops 4194304 | bytes 4194304 | tf_op jit(solution)/shard_map/local/pallas_call | solution.py:258
  21.3 0.0 collective-permute-done.near_ref
  21.3 3.3 %collective-permute-done.1.far_ref = bf16[5,8,1024]{2,1,0:T(8,128)(2,1)S(1)} collective-permute-done((bf16[5,8,1024]{2,1,0:T(8,128)(2,1)S(1)}, bf16[5,8,1024]{2,1,0:T(8,128)(2,1)S(1)}, u32[]{:S(2)}, u32[]{:S(2)}) %collective-permute-start.1) | collective-permute-done | bytes 81952 | tf_op jit(solution)/shard_map/ppermute | solution.py:256
  24.6 0.0 copy-start
  24.6 0.0 copy-start.1
  24.6 0.0 copy-start.2
  24.6 0.2 finish.1
  24.8 10.3 %all_to_all.10.data_ref = bf16[16,48,128]{2,1,0:T(8,128)(2,1)S(1)} all-to-all(bf16[16,48,128]{2,1,0:T(8,128)(2,1)S(1)} %finish.1), channel_id=1, replica_groups=mesh['lev'=16,'lat'=64] {'lev'}, dimensions={0} | all-to-all | bytes 393216 | tf_op jit(solution)/shard_map/all_to_all | solution.py:288
  35.1 0.0 copy-done
  35.1 0.0 copy-done.1
  35.1 0.0 copy-done.2
  35.1 1.3 %physics.1 = bf16[16,48,128]{2,1,0:T(8,128)(2,1)S(1)} custom-call(bf16[16,48,128]{2,1,0:T(8,128)(2,1)S(1)} %all_to_all.10.data_ref, bf16[256,256]{1,0:T(8,128)(2,1)S(1)} %get-tuple-element.28.high_ref, bf16[256,256]{1,0:T(8,128)(2,1)S(1)} %get-tuple-element.29.low_ref, f32[192,128]{1,0:T(8,128)S(1)} %get-tuple-element.30.mask_ref, ...), custom_call_target="tpu_custom_call" | custom-call | flops 1073741824 | bytes 4194304 | tf_op jit(solution)/shard_map/physics/pallas_call | solution.py:289
  36.5 11.2 %all_to_all.11.data_ref = bf16[16,48,128]{2,1,0:T(8,128)(2,1)S(1)} all-to-all(bf16[16,48,128]{2,1,0:T(8,128)(2,1)S(1)} %physics.1), channel_id=1, replica_groups=mesh['lev'=16,'lat'=64] {'lev'}, dimensions={0} | all-to-all | bytes 393216 | tf_op jit(solution)/shard_map/all_to_all | solution.py:298
  47.6 0.8 %unpack.1 = f32[4,3,8,1024]{3,2,1,0:T(8,128)} custom-call(bf16[16,48,128]{2,1,0:T(8,128)(2,1)S(1)} %all_to_all.11.data_ref), custom_call_target="tpu_custom_call" | custom-call | flops 262144 | bytes 1048576 | tf_op jit(solution)/shard_map/unpack/pallas_call | solution.py:299
Async XLA Ops:
  1.2 20.1 %collective-permute-start = (bf16[5,8,1024]{2,1,0:T(8,128)(2,1)S(1)}, bf16[5,8,1024]{2,1,0:T(8,128)(2,1)S(1)}, u32[]{:S(2)}, u32[]{:S(2)}) collective-permute-start(bf16[5,8,1024]{2,1,0:T(8,128)(2,1)S(1)} %get-tuple-element.22), channel_id=1, source_target_pairs={{0,1},{2,3},{4,5},{6,7},{8,9},{10,11},{12,13},{14,15},{16,17},{18,... | collective-permute-start | bytes 245768 | tf_op jit(solution)/shard_map/ppermute | solution.py:257
  17.2 7.4 %collective-permute-start.1 = (bf16[5,8,1024]{2,1,0:T(8,128)(2,1)S(1)}, bf16[5,8,1024]{2,1,0:T(8,128)(2,1)S(1)}, u32[]{:S(2)}, u32[]{:S(2)}) collective-permute-start(bf16[5,8,1024]{2,1,0:T(8,128)(2,1)S(1)} %get-tuple-element.23), channel_id=1, source_target_pairs={{1,2},{3,4},{5,6},{7,8},{9,10},{11,12},{13,14},{15,16},{17,18},{19... | collective-permute-start | bytes 245768 | tf_op jit(solution)/shard_map/ppermute | solution.py:256
  24.6 10.5 %copy-start = (bf16[1024,1024]{1,0:T(8,128)(2,1)S(1)}, bf16[1024,1024]{1,0:T(8,128)(2,1)}, u32[]{:S(2)}) copy-start(bf16[1024,1024]{1,0:T(8,128)(2,1)} %w_mid_ref.1) | copy-start | bytes 6291460
  24.6 10.5 %copy-start.1 = (bf16[512,1024]{1,0:T(8,128)(2,1)S(1)}, bf16[512,1024]{1,0:T(8,128)(2,1)}, u32[]{:S(2)}) copy-start(bf16[512,1024]{1,0:T(8,128)(2,1)} %w_in_ref.1) | copy-start | bytes 3145732
  24.6 10.5 %copy-start.2 = (bf16[1024,512]{1,0:T(8,128)(2,1)S(1)}, bf16[1024,512]{1,0:T(8,128)(2,1)}, u32[]{:S(2)}) copy-start(bf16[1024,512]{1,0:T(8,128)(2,1)} %w_out_ref.1) | copy-start | bytes 3145732

commit v4 on v3

--- a/solution.py
+++ b/solution.py
@@ -5,6 +5,7 @@
 from jax.experimental.pallas import tpu as pltpu
 from jax.sharding import PartitionSpec as P
 
+
 NB = 8
 F32 = jnp.float32
 BF16 = jnp.bfloat16
@@ -31,7 +32,10 @@
     return lax.rem(lax.axis_index("lat"), 2) == 0
 
 
-def load_kernel(state_ref, east_ref, north_ref, cells_ref, easterly_ref, northerly_ref, near_ref, far_ref, sems):
+def load_kernel(
+    state_ref, east_ref, north_ref, weight_ref, list_ref,
+    cells_ref, easterly_ref, northerly_ref, weight_out, list_out, near_ref, far_ref, sems,
+):
     fields, rows = state_ref.shape[:2]
     last = rows - 1
 
@@ -49,6 +53,8 @@
     rest = [
         bring(state_ref.at[:, 1:last], cells_ref.at[:, 1:last], 3),
         bring(east_ref, easterly_ref, 5),
+        bring(weight_ref, weight_out, 6),
+        bring(list_ref, list_out, 7),
     ]
     for copy in first:
         copy.wait()
@@ -78,16 +84,8 @@
 
 def local_kernel(
     state_ref, east_ref, north_ref, list_ref, count_ref, weight_ref,
-    out_ref, high_ref, low_ref, mask_ref, order, weight, sems,
+    out_ref, high_ref, low_ref, mask_ref,
 ):
-    copies = [
-        pltpu.make_async_copy(source, target, sems.at[k])
-        for k, (source, target) in enumerate(
-            ((list_ref, order), (weight_ref, weight))
-        )
-    ]
-    for copy in copies:
-        copy.start()
     fields, rows, _, width = state_ref.shape
     for f in range(fields):
         below_flux = None
@@ -105,22 +103,20 @@
                 below_flux = jnp.maximum(wind, 0.0) * cells + jnp.minimum(wind, 0.0) * state_ref[f, j + 1]
                 value = value - below_flux
             out_ref[f, j] = value
-    for copy in copies:
-        copy.wait()
-    pair = pair_remap(weight[...])
+    pair = pair_remap(weight_ref[...])
     high = pair.astype(BF16)
     high_ref[...] = high
     low_ref[...] = (pair - high.astype(F32)).astype(BF16)
-    bits = jnp.int32(0)
-    count = count_ref[0, 0]
-    for s in range(NB):
-        bits = bits + jnp.where(s < count, jnp.left_shift(jnp.int32(1), order[0, 0, s]), 0)
     odd = lax.rem(lax.axis_index("lev"), 2)
     place = lax.broadcasted_iota(jnp.int32, mask_ref.shape, 0)
     column = jnp.where(place < 128, place + 64 * odd, place - 128 * odd)
     block = jnp.right_shift(column * 2731, 16)
-    active = jnp.bitwise_and(jnp.right_shift(jnp.full(mask_ref.shape, bits), block), 1)
-    mask_ref[...] = active.astype(F32)
+    count = count_ref[0, 0]
+    active = jnp.zeros(mask_ref.shape, F32)
+    for s in range(NB):
+        listed = jnp.where(s < count, list_ref[0, :, s : s + 1], -1)
+        active = jnp.where(block == listed, 1.0, active)
+    mask_ref[...] = active
 
 
 def finish_kernel(local_ref, state_ref, north_ref, near_ref, far_ref, out_ref):
@@ -198,7 +194,6 @@
 
 
 def unpack_kernel(data_ref, out_ref):
-    fields = out_ref.shape[0]
     lane = lax.broadcasted_iota(jnp.int32, (16, 128), 1)
     low = lane < 64
 
@@ -237,22 +232,24 @@
     hbm = pl.BlockSpec(memory_space=pltpu.HBM)
     levels = lev_dev * lev_count
     col_count = lat_rows * lon_cells // lev_count
-    held_cells, held_east, held_north, near, far = pl.pallas_call(
+    held_cells, held_east, held_north, held_weight, held_list, near, far = pl.pallas_call(
         load_kernel,
         out_shape=[
             jax.ShapeDtypeStruct(cells.shape, F32),
             jax.ShapeDtypeStruct(east.shape, F32),
             jax.ShapeDtypeStruct(north.shape, F32),
+            jax.ShapeDtypeStruct(remap_weight.shape, F32),
+            jax.ShapeDtypeStruct(block_list.shape, jnp.int32),
             jax.ShapeDtypeStruct((fields + 1, *edge), BF16),
             jax.ShapeDtypeStruct((fields + 1, *edge), BF16),
         ],
-        in_specs=[hbm] * 3,
-        out_specs=[whole()] * 5,
-        scratch_shapes=[pltpu.SemaphoreType.DMA((6,))],
+        in_specs=[hbm] * 5,
+        out_specs=[whole()] * 7,
+        scratch_shapes=[pltpu.SemaphoreType.DMA((8,))],
         compiler_params=params(4),
         cost_estimate=cost(1 << 17, 1 << 21),
         name="load",
-    )(*map(in_hbm, (cells, east, north)))
+    )(*map(in_hbm, (cells, east, north, remap_weight, block_list)))
     far = lax.ppermute(far, "lat", pairs(1, lat_count))
     near = lax.ppermute(near, "lat", pairs(0, lat_count))
     local, high, low, mask = pl.pallas_call(
@@ -263,17 +260,12 @@
             jax.ShapeDtypeStruct((2 * levels, 2 * levels), BF16),
             jax.ShapeDtypeStruct((col_count, 128), F32),
         ],
-        in_specs=[whole()] * 3 + [hbm, smem, hbm],
+        in_specs=[whole()] * 4 + [smem, whole()],
         out_specs=[whole()] * 4,
-        scratch_shapes=[
-            pltpu.SMEM(block_list.shape, jnp.int32),
-            VM(remap_weight.shape, F32),
-            pltpu.SemaphoreType.DMA((2,)),
-        ],
         compiler_params=params(4),
         cost_estimate=cost(1 << 22, 1 << 22),
         name="local",
-    )(held_cells, held_east, held_north, in_hbm(block_list), block_count, in_hbm(remap_weight))
+    )(held_cells, held_east, held_north, held_list, block_count, held_weight)
     chunk = (lev_count, fields * lev_dev * lat_rows * lon_cells // lev_count // 128, 128)
     packed = pl.pallas_call(
         finish_kernel,

time: 48.7 us -> 48.4 us (level)
  waiting for transfers between devices: 3.31 us -> 3.89 us
  Pallas kernels: 5.02 us -> 4.48 us
    ppermute x1, waiting for transfers between devices: 3.3 us -> 3.88 us  [per_device(): far = lax.ppermute(far, 'lat', pairs(1, lat_count))]
    pallas_call x1, Pallas kernels: 1.5 us -> 0.92 us  [per_device(): pl.pallas_call(local_kernel, out_shape=[jax.ShapeDtypeStruct(cells.shape,...]
  transfers between devices with their start and end apart: 2 -> 2, of which waited for: 1 -> 1; matrix products, arithmetic and copies ran while one was open for 0% -> 0% of each run, Pallas kernels for 3% -> 2%
where the time goes in v4:
time: 48.4 us; the launch traced here: 48.2 us
  blocking collectives  21.2 us (44%)
  starting transfers between devices  17.9 us (37%)
  Pallas kernels  4.48 us (9%)
  waiting for transfers between devices  3.89 us (8%)
  between operations  0.7 us (1%)
    ppermute x1, starting transfers between devices, per_device(): near = lax.ppermute(near, 'lat', pairs(0, lat_count))  16 us
    all_to_all x1, blocking collectives, per_device(): lax.all_to_all(finished, 'lev', split_axis=0, concat_axis=0, tiled=True)  10.9 us
    all_to_all x1, blocking collectives, per_device(): lax.all_to_all(packed, 'lev', split_axis=0, concat_axis=0, tiled=True)  10.3 us
    ppermute x1, waiting for transfers between devices, per_device(): far = lax.ppermute(far, 'lat', pairs(1, lat_count))  3.88 us
    ppermute x1, starting transfers between devices, per_device(): far = lax.ppermute(far, 'lat', pairs(1, lat_count))  1.92 us
    pallas_call x1, Pallas kernels, per_device(): pl.pallas_call(physics_kernel, out_shape=jax.ShapeDtypeStruct(chunk, BF16...  1.36 us
    pallas_call x1, Pallas kernels, per_device(): pl.pallas_call(load_kernel, out_shape=[jax.ShapeDtypeStruct(cells.shape,...  1.21 us
  transfers between devices with their start and end apart: 2, of which 1 were waited for; matrix products, arithmetic and copies ran while one was open for 0% of the time, Pallas kernels for 2%

profile of v4, /device:TPU:1, one launch (start us, length us, event | category | flops | bytes accessed | tf_op | source)
XLA Modules:
  0.0 48.2 jit_solution(717191707602390653)
XLA Ops:
  0.0 1.2 %load.1 = (f32[4,3,8,1024]{3,2,1,0:T(8,128)S(1)}, f32[3,8,1024]{2,1,0:T(8,128)S(1)}, f32[3,8,1024]{2,1,0:T(8,128)S(1)}, f32[128,128]{1,0:T(8,128)S(1)}, s32[1,1,...) custom-call(f32[4,3,8,1024]{3,2,1,0:T(8,128)} %bitcast.4, f32[3,8,1024]{2,1,0:T(8,128)} %bitcast.5, ...), custom_call_target="tpu_custom_call" | custom-call | flops 131072 | bytes 2097152 | tf_op jit(solution)/shard_map/load/pallas_call | solution.py:235
  1.2 16.0 %collective-permute-start = (bf16[5,8,1024]{2,1,0:T(8,128)(2,1)S(1)}, bf16[5,8,1024]{2,1,0:T(8,128)(2,1)S(1)}, u32[]{:S(2)}, u32[]{:S(2)}) collective-permute-start(bf16[5,8,1024]{2,1,0:T(8,128)(2,1)S(1)} %get-tuple-element.26), channel_id=1, source_target_pairs={{0,1},{2,3},{4,5},{6,7},{8,9},{10,11},{12,13},{14,15},{16,17},{18,... | collective-permute-start | bytes 245768 | tf_op jit(solution)/shard_map/ppermute | solution.py:254
  17.2 1.9 %collective-permute-start.1 = (bf16[5,8,1024]{2,1,0:T(8,128)(2,1)S(1)}, bf16[5,8,1024]{2,1,0:T(8,128)(2,1)S(1)}, u32[]{:S(2)}, u32[]{:S(2)}) collective-permute-start(bf16[5,8,1024]{2,1,0:T(8,128)(2,1)S(1)} %get-tuple-element.27), channel_id=1, source_target_pairs={{1,2},{3,4},{5,6},{7,8},{9,10},{11,12},{13,14},{15,16},{17,18},{19... | collective-permute-start | bytes 245768 | tf_op jit(solution)/shard_map/ppermute | solution.py:253
  19.8 0.9 %local.1 = (f32[4,3,8,1024]{3,2,1,0:T(8,128)S(1)}, bf16[256,256]{1,0:T(8,128)(2,1)S(1)}, bf16[256,256]{1,0:T(8,128)(2,1)S(1)}, f32[192,128]{1,0:T(8,128)S(1)}) custom-call(f32[4,3,8,1024]{3,2,1,0:T(8,128)S(1)} %get-tuple-element.20.state_ref, f32[3,8,1024]{2,1,0:T(8,128)S(1)} %get-tuple-element.21.east_ref, f32[3,8,1024]{2,1,0:T(8,128)S(1)} %get-tuple-element.22.north_ref, ...), custom_call_target="tpu_custom_call" | custom-call | flops 4194304 | bytes 4194304 | tf_op jit(solution)/shard_map/local/pallas_call | solution.py:255
  20.7 0.0 collective-permute-done.near_ref
  20.8 3.9 %collective-permute-done.1.far_ref = bf16[5,8,1024]{2,1,0:T(8,128)(2,1)S(1)} collective-permute-done((bf16[5,8,1024]{2,1,0:T(8,128)(2,1)S(1)}, bf16[5,8,1024]{2,1,0:T(8,128)(2,1)S(1)}, u32[]{:S(2)}, u32[]{:S(2)}) %collective-permute-start.1) | collective-permute-done | bytes 81952 | tf_op jit(solution)/shard_map/ppermute | solution.py:253
  24.6 0.0 copy-start
  24.6 0.0 copy-start.1
  24.6 0.0 copy-start.2
  24.6 0.2 finish.1
  24.8 10.3 %all_to_all.10.data_ref = bf16[16,48,128]{2,1,0:T(8,128)(2,1)S(1)} all-to-all(bf16[16,48,128]{2,1,0:T(8,128)(2,1)S(1)} %finish.1), channel_id=1, replica_groups=mesh['lev'=16,'lat'=64] {'lev'}, dimensions={0} | all-to-all | bytes 393216 | tf_op jit(solution)/shard_map/all_to_all | solution.py:280
  35.1 0.0 copy-done
  35.1 0.0 copy-done.1
  35.1 0.0 copy-done.2
  35.1 1.4 %physics.1 = bf16[16,48,128]{2,1,0:T(8,128)(2,1)S(1)} custom-call(bf16[16,48,128]{2,1,0:T(8,128)(2,1)S(1)} %all_to_all.10.data_ref, bf16[256,256]{1,0:T(8,128)(2,1)S(1)} %get-tuple-element.32.high_ref, bf16[256,256]{1,0:T(8,128)(2,1)S(1)} %get-tuple-element.33.low_ref, f32[192,128]{1,0:T(8,128)S(1)} %get-tuple-element.34.mask_ref, ...), custom_call_target="tpu_custom_call" | custom-call | flops 1073741824 | bytes 4194304 | tf_op jit(solution)/shard_map/physics/pallas_call | solution.py:281
  36.5 10.9 %all_to_all.11.data_ref = bf16[16,48,128]{2,1,0:T(8,128)(2,1)S(1)} all-to-all(bf16[16,48,128]{2,1,0:T(8,128)(2,1)S(1)} %physics.1), channel_id=1, replica_groups=mesh['lev'=16,'lat'=64] {'lev'}, dimensions={0} | all-to-all | bytes 393216 | tf_op jit(solution)/shard_map/all_to_all | solution.py:290
  47.4 0.8 %unpack.1 = f32[4,3,8,1024]{3,2,1,0:T(8,128)} custom-call(bf16[16,48,128]{2,1,0:T(8,128)(2,1)S(1)} %all_to_all.11.data_ref), custom_call_target="tpu_custom_call" | custom-call | flops 262144 | bytes 1048576 | tf_op jit(solution)/shard_map/unpack/pallas_call | solution.py:291
Async XLA Ops:
  1.2 19.5 %collective-permute-start = (bf16[5,8,1024]{2,1,0:T(8,128)(2,1)S(1)}, bf16[5,8,1024]{2,1,0:T(8,128)(2,1)S(1)}, u32[]{:S(2)}, u32[]{:S(2)}) collective-permute-start(bf16[5,8,1024]{2,1,0:T(8,128)(2,1)S(1)} %get-tuple-element.26), channel_id=1, source_target_pairs={{0,1},{2,3},{4,5},{6,7},{8,9},{10,11},{12,13},{14,15},{16,17},{18,... | collective-permute-start | bytes 245768 | tf_op jit(solution)/shard_map/ppermute | solution.py:254
  17.2 7.4 %collective-permute-start.1 = (bf16[5,8,1024]{2,1,0:T(8,128)(2,1)S(1)}, bf16[5,8,1024]{2,1,0:T(8,128)(2,1)S(1)}, u32[]{:S(2)}, u32[]{:S(2)}) collective-permute-start(bf16[5,8,1024]{2,1,0:T(8,128)(2,1)S(1)} %get-tuple-element.27), channel_id=1, source_target_pairs={{1,2},{3,4},{5,6},{7,8},{9,10},{11,12},{13,14},{15,16},{17,18},{19... | collective-permute-start | bytes 245768 | tf_op jit(solution)/shard_map/ppermute | solution.py:253
  24.6 10.5 %copy-start = (bf16[1024,1024]{1,0:T(8,128)(2,1)S(1)}, bf16[1024,1024]{1,0:T(8,128)(2,1)}, u32[]{:S(2)}) copy-start(bf16[1024,1024]{1,0:T(8,128)(2,1)} %w_mid_ref.1) | copy-start | bytes 6291460
  24.6 10.5 %copy-start.1 = (bf16[512,1024]{1,0:T(8,128)(2,1)S(1)}, bf16[512,1024]{1,0:T(8,128)(2,1)}, u32[]{:S(2)}) copy-start(bf16[512,1024]{1,0:T(8,128)(2,1)} %w_in_ref.1) | copy-start | bytes 3145732
  24.6 10.5 %copy-start.2 = (bf16[1024,512]{1,0:T(8,128)(2,1)S(1)}, bf16[1024,512]{1,0:T(8,128)(2,1)}, u32[]{:S(2)}) copy-start(bf16[1024,512]{1,0:T(8,128)(2,1)} %w_out_ref.1) | copy-start | bytes 3145732

commit v5 on v4

--- a/solution.py
+++ b/solution.py
@@ -32,39 +32,26 @@
     return lax.rem(lax.axis_index("lat"), 2) == 0
 
 
-def load_kernel(
-    state_ref, east_ref, north_ref, weight_ref, list_ref,
-    cells_ref, easterly_ref, northerly_ref, weight_out, list_out, near_ref, far_ref, sems,
-):
+def edge_kernel(state_ref, north_ref, near_ref, far_ref, rows_ref, winds_ref, sems):
     fields, rows = state_ref.shape[:2]
     last = rows - 1
-
-    def bring(source, target, k):
-        copy = pltpu.make_async_copy(source, target, sems.at[k])
-        copy.start()
-        return copy
-
-    first = [
-        bring(state_ref.at[:, last], cells_ref.at[:, last], 0),
-        bring(north_ref.at[last], northerly_ref.at[last], 1),
-        bring(state_ref.at[:, 0], cells_ref.at[:, 0], 2),
-        bring(north_ref.at[:last], northerly_ref.at[:last], 4),
-    ]
-    rest = [
-        bring(state_ref.at[:, 1:last], cells_ref.at[:, 1:last], 3),
-        bring(east_ref, easterly_ref, 5),
-        bring(weight_ref, weight_out, 6),
-        bring(list_ref, list_out, 7),
-    ]
-    for copy in first:
+    even = even_band()
+    near_row = jnp.where(even, last, 0)
+    copies = []
+    for k, row in enumerate((last - near_row, near_row)):
+        for source, target, sem in (
+            (state_ref.at[:, row], rows_ref.at[k], sems.at[k, 0]),
+            (north_ref.at[row], winds_ref.at[k], sems.at[k, 1]),
+        ):
+            copy = pltpu.make_async_copy(source, target, sem)
+            copy.start()
+            copies.append(copy)
+    for copy in copies:
         copy.wait()
-    near_row = jnp.where(even_band(), last, 0)
-    for edge_ref, row in ((near_ref, near_row), (far_ref, last - near_row)):
+    for k, edge_ref in enumerate((far_ref, near_ref)):
         for f in range(fields):
-            edge_ref[f] = cells_ref[f, row].astype(BF16)
-        edge_ref[fields] = northerly_ref[row].astype(BF16)
-    for copy in rest:
-        copy.wait()
+            edge_ref[f] = rows_ref[k, f].astype(BF16)
+        edge_ref[fields] = winds_ref[k].astype(BF16)
 
 
 def pair_remap(weight):
@@ -193,24 +180,31 @@
     put(32, jnp.concatenate([finished[128:, :256], finished[128:, 256:]], axis=0))
 
 
-def unpack_kernel(data_ref, out_ref):
-    lane = lax.broadcasted_iota(jnp.int32, (16, 128), 1)
-    low = lane < 64
-
-    def put(v, pair, value):
-        j, k = divmod(v, 8)
-        for f in range(2):
-            out_ref[2 * pair + f, j, :, k * 128 : (k + 1) * 128] = value[8 * f : 8 * f + 8]
-
-    for p in range(8):
-        a = data_ref[2 * p].astype(F32)
-        b = data_ref[2 * p + 1].astype(F32)
-        for pair in range(2):
-            put(3 * p, pair, a[16 * pair : 16 * pair + 16])
-            put(3 * p + 2, pair, b[16 * pair : 16 * pair + 16])
-        end_a, end_b = a[32:], b[32:]
-        put(3 * p + 1, 0, jnp.where(low, end_a, pltpu.roll(end_b, 64, 1)))
-        put(3 * p + 1, 1, jnp.where(low, pltpu.roll(end_a, 64, 1), end_b))
+def unpack_kernel(data_ref, out_ref, buffer, sems):
+    fields = out_ref.shape[0]
+    low = lax.broadcasted_iota(jnp.int32, (16, 128), 1) < 64
+    copies = []
+    for pair in range(fields // 2):
+
+        def put(v, value):
+            j, k = divmod(v, 8)
+            for f in range(2):
+                buffer[2 * pair + f, j, :, k * 128 : (k + 1) * 128] = value[8 * f : 8 * f + 8]
+
+        for p in range(8):
+            put(3 * p, data_ref[2 * p, 16 * pair : 16 * pair + 16].astype(F32))
+            put(3 * p + 2, data_ref[2 * p + 1, 16 * pair : 16 * pair + 16].astype(F32))
+            end_a, end_b = (data_ref[2 * p + i, 32:].astype(F32) for i in range(2))
+            if pair == 0:
+                put(3 * p + 1, jnp.where(low, end_a, pltpu.roll(end_b, 64, 1)))
+            else:
+                put(3 * p + 1, jnp.where(low, pltpu.roll(end_a, 64, 1), end_b))
+        ready = pl.ds(2 * pair, 2)
+        copy = pltpu.make_async_copy(buffer.at[ready], out_ref.at[ready], sems.at[pair])
+        copy.start()
+        copies.append(copy)
+    for copy in copies:
+        copy.wait()
 
 
 def pairs(start, count):
@@ -232,24 +226,20 @@
     hbm = pl.BlockSpec(memory_space=pltpu.HBM)
     levels = lev_dev * lev_count
     col_count = lat_rows * lon_cells // lev_count
-    held_cells, held_east, held_north, held_weight, held_list, near, far = pl.pallas_call(
-        load_kernel,
-        out_shape=[
-            jax.ShapeDtypeStruct(cells.shape, F32),
-            jax.ShapeDtypeStruct(east.shape, F32),
-            jax.ShapeDtypeStruct(north.shape, F32),
-            jax.ShapeDtypeStruct(remap_weight.shape, F32),
-            jax.ShapeDtypeStruct(block_list.shape, jnp.int32),
-            jax.ShapeDtypeStruct((fields + 1, *edge), BF16),
-            jax.ShapeDtypeStruct((fields + 1, *edge), BF16),
+    near, far = pl.pallas_call(
+        edge_kernel,
+        out_shape=[jax.ShapeDtypeStruct((fields + 1, *edge), BF16)] * 2,
+        in_specs=[hbm] * 2,
+        out_specs=[whole()] * 2,
+        scratch_shapes=[
+            VM((2, fields, *edge), F32),
+            VM((2, *edge), F32),
+            pltpu.SemaphoreType.DMA((2, 2)),
         ],
-        in_specs=[hbm] * 5,
-        out_specs=[whole()] * 7,
-        scratch_shapes=[pltpu.SemaphoreType.DMA((8,))],
         compiler_params=params(4),
-        cost_estimate=cost(1 << 17, 1 << 21),
-        name="load",
-    )(*map(in_hbm, (cells, east, north, remap_weight, block_list)))
+        cost_estimate=cost(1 << 33, 1 << 21),
+        name="edges",
+    )(*map(in_hbm, (cells, north)))
     far = lax.ppermute(far, "lat", pairs(1, lat_count))
     near = lax.ppermute(near, "lat", pairs(0, lat_count))
     local, high, low, mask = pl.pallas_call(
@@ -265,7 +255,7 @@
         compiler_params=params(4),
         cost_estimate=cost(1 << 22, 1 << 22),
         name="local",
-    )(held_cells, held_east, held_north, held_list, block_count, held_weight)
+    )(cells, east, north, block_list, block_count, remap_weight)
     chunk = (lev_count, fields * lev_dev * lat_rows * lon_cells // lev_count // 128, 128)
     packed = pl.pallas_call(
         finish_kernel,
@@ -275,7 +265,7 @@
         compiler_params=params(4),
         cost_estimate=cost(1 << 34, 1 << 20),
         name="finish",
-    )(local, held_cells, held_north, near, far)
+    )(local, cells, north, near, far)
     packed, high, low, mask = lax.optimization_barrier((packed, high, low, mask))
     columns = lax.all_to_all(packed, "lev", split_axis=0, concat_axis=0, tiled=True)
     finished = pl.pallas_call(
@@ -292,7 +282,8 @@
         unpack_kernel,
         out_shape=jax.ShapeDtypeStruct(cells.shape, F32),
         in_specs=[whole()],
-        out_specs=whole(),
+        out_specs=hbm,
+        scratch_shapes=[VM(cells.shape, F32), pltpu.SemaphoreType.DMA((2,))],
         compiler_params=params(4),
         cost_estimate=cost(1 << 18, 1 << 20),
         name="unpack",

time: 48.4 us -> 48.5 us (level)
  no operation moved by 1% of the time
where the time goes in v5:
time: 48.5 us; the launch traced here: 48.2 us
  blocking collectives  21.3 us (44%)
  starting transfers between devices  17.9 us (37%)
  Pallas kernels  4.37 us (9%)
  waiting for transfers between devices  3.82 us (8%)
  between operations  0.76 us (2%)
    ppermute x1, starting transfers between devices, per_device(): near = lax.ppermute(near, 'lat', pairs(0, lat_count))  16 us
    all_to_all x1, blocking collectives, per_device(): lax.all_to_all(finished, 'lev', split_axis=0, concat_axis=0, tiled=True)  11 us
    all_to_all x1, blocking collectives, per_device(): lax.all_to_all(packed, 'lev', split_axis=0, concat_axis=0, tiled=True)  10.3 us
    ppermute x1, waiting for transfers between devices, per_device(): far = lax.ppermute(far, 'lat', pairs(1, lat_count))  3.82 us
    ppermute x1, starting transfers between devices, per_device(): far = lax.ppermute(far, 'lat', pairs(1, lat_count))  1.92 us
    pallas_call x1, Pallas kernels, per_device(): pl.pallas_call(physics_kernel, out_shape=jax.ShapeDtypeStruct(chunk, BF16...  1.35 us
    pallas_call x1, Pallas kernels, per_device(): pl.pallas_call(edge_kernel, out_shape=[jax.ShapeDtypeStruct((fields + 1,...  1.11 us
  transfers between devices with their start and end apart: 2, of which 1 were waited for; matrix products, arithmetic and copies ran while one was open for 0% of the time, Pallas kernels for 2%

profile of v5, /device:TPU:1, one launch (start us, length us, event | category | flops | bytes accessed | tf_op | source)
XLA Modules:
  0.0 48.2 jit_solution(1071475482235149225)
XLA Ops:
  0.0 0.0 copy-start.3
  0.0 0.0 copy-start.4
  0.0 0.0 copy-start.5
  0.0 0.0 copy-start.6
  0.0 0.0 copy-start.7
  0.0 1.1 %edges.1 = (bf16[5,8,1024]{2,1,0:T(8,128)(2,1)S(1)}, bf16[5,8,1024]{2,1,0:T(8,128)(2,1)S(1)}) custom-call(f32[4,3,8,1024]{3,2,1,0:T(8,128)} %bitcast.4, f32[3,8,1024]{2,1,0:T(8,128)} %bitcast.8), custom_call_target="tpu_custom_call" | custom-call | flops 8589934592 | bytes 2097152 | tf_op jit(solution)/shard_map/edges/pallas_call | solution.py:229
  1.1 16.0 %collective-permute-start = (bf16[5,8,1024]{2,1,0:T(8,128)(2,1)S(1)}, bf16[5,8,1024]{2,1,0:T(8,128)(2,1)S(1)}, u32[]{:S(2)}, u32[]{:S(2)}) collective-permute-start(bf16[5,8,1024]{2,1,0:T(8,128)(2,1)S(1)} %get-tuple-element.16), channel_id=1, source_target_pairs={{0,1},{2,3},{4,5},{6,7},{8,9},{10,11},{12,13},{14,15},{16,17},{18,... | collective-permute-start | bytes 245768 | tf_op jit(solution)/shard_map/ppermute | solution.py:244
  17.2 1.9 %collective-permute-start.1 = (bf16[5,8,1024]{2,1,0:T(8,128)(2,1)S(1)}, bf16[5,8,1024]{2,1,0:T(8,128)(2,1)S(1)}, u32[]{:S(2)}, u32[]{:S(2)}) collective-permute-start(bf16[5,8,1024]{2,1,0:T(8,128)(2,1)S(1)} %get-tuple-element.17), channel_id=1, source_target_pairs={{1,2},{3,4},{5,6},{7,8},{9,10},{11,12},{13,14},{15,16},{17,18},{19... | collective-permute-start | bytes 245768 | tf_op jit(solution)/shard_map/ppermute | solution.py:243
  19.7 0.0 copy-done.3
  19.7 0.0 copy-done.4
  19.8 0.0 copy-done.5
  19.8 0.0 copy-done.6
  19.8 0.0 copy-done.7
  19.8 0.9 %local.1 = (f32[4,3,8,1024]{3,2,1,0:T(8,128)S(1)}, bf16[256,256]{1,0:T(8,128)(2,1)S(1)}, bf16[256,256]{1,0:T(8,128)(2,1)S(1)}, f32[192,128]{1,0:T(8,128)S(1)}) custom-call(f32[4,3,8,1024]{3,2,1,0:T(8,128)S(1)} %bitcast.5, f32[3,8,1024]{2,1,0:T(8,128)S(1)} %bitcast.7, f32[3,8,1024]{2,1,0:T(8,128)S(1)} %bitcast.9, s32[1,1,8]{2,1,0:T(1,128)S(1)} %copy-done.7, ...), custom_call_target="tpu_custom_call" | custom-call | flops 4194304 | bytes 4194304 | tf_op jit(solution)/shard_map/local/pallas_call | solution.py:245
  20.7 0.0 collective-permute-done.near_ref
  20.7 3.8 %collective-permute-done.1.far_ref = bf16[5,8,1024]{2,1,0:T(8,128)(2,1)S(1)} collective-permute-done((bf16[5,8,1024]{2,1,0:T(8,128)(2,1)S(1)}, bf16[5,8,1024]{2,1,0:T(8,128)(2,1)S(1)}, u32[]{:S(2)}, u32[]{:S(2)}) %collective-permute-start.1) | collective-permute-done | bytes 81952 | tf_op jit(solution)/shard_map/ppermute | solution.py:243
  24.5 0.0 copy-start
  24.6 0.0 copy-start.1
  24.6 0.0 copy-start.2
  24.6 0.2 finish.1
  24.7 10.3 %all_to_all.10.data_ref = bf16[16,48,128]{2,1,0:T(8,128)(2,1)S(1)} all-to-all(bf16[16,48,128]{2,1,0:T(8,128)(2,1)S(1)} %finish.1), channel_id=1, replica_groups=mesh['lev'=16,'lat'=64] {'lev'}, dimensions={0} | all-to-all | bytes 393216 | tf_op jit(solution)/shard_map/all_to_all | solution.py:270
  35.0 0.0 copy-done
  35.0 0.0 copy-done.1
  35.0 0.0 copy-done.2
  35.0 1.3 %physics.1 = bf16[16,48,128]{2,1,0:T(8,128)(2,1)S(1)} custom-call(bf16[16,48,128]{2,1,0:T(8,128)(2,1)S(1)} %all_to_all.10.data_ref, bf16[256,256]{1,0:T(8,128)(2,1)S(1)} %get-tuple-element.22.high_ref, bf16[256,256]{1,0:T(8,128)(2,1)S(1)} %get-tuple-element.23.low_ref, f32[192,128]{1,0:T(8,128)S(1)} %get-tuple-element.24.mask_ref, ...), custom_call_target="tpu_custom_call" | custom-call | flops 1073741824 | bytes 4194304 | tf_op jit(solution)/shard_map/physics/pallas_call | solution.py:271
  36.4 11.0 %all_to_all.11.data_ref = bf16[16,48,128]{2,1,0:T(8,128)(2,1)S(1)} all-to-all(bf16[16,48,128]{2,1,0:T(8,128)(2,1)S(1)} %physics.1), channel_id=1, replica_groups=mesh['lev'=16,'lat'=64] {'lev'}, dimensions={0} | all-to-all | bytes 393216 | tf_op jit(solution)/shard_map/all_to_all | solution.py:280
  47.4 0.8 %unpack.1 = f32[4,3,8,1024]{3,2,1,0:T(8,128)} custom-call(bf16[16,48,128]{2,1,0:T(8,128)(2,1)S(1)} %all_to_all.11.data_ref), custom_call_target="tpu_custom_call" | custom-call | flops 262144 | bytes 1048576 | tf_op jit(solution)/shard_map/unpack/pallas_call | solution.py:281
Async XLA Ops:
  0.0 19.7 %copy-start.3 = (f32[4,8,3,1024]{3,1,2,0:T(8,128)S(1)}, f32[4,8,3,1024]{3,1,2,0:T(8,128)}, u32[]{:S(2)}) copy-start(f32[4,8,3,1024]{3,1,2,0:T(8,128)} %param.9) | copy-start | bytes 1179652
  0.0 19.7 %copy-start.4 = (f32[8,3,1024]{2,0,1:T(8,128)S(1)}, f32[8,3,1024]{2,0,1:T(8,128)}, u32[]{:S(2)}) copy-start(f32[8,3,1024]{2,0,1:T(8,128)} %param.10) | copy-start | bytes 294916
  0.0 19.8 %copy-start.5 = (f32[8,3,1024]{2,0,1:T(8,128)S(1)}, f32[8,3,1024]{2,0,1:T(8,128)}, u32[]{:S(2)}) copy-start(f32[8,3,1024]{2,0,1:T(8,128)} %param.11) | copy-start | bytes 294916
  0.0 19.8 %copy-start.6 = (f32[128,128]{1,0:T(8,128)S(1)}, f32[128,128]{1,0:T(8,128)}, u32[]{:S(2)}) copy-start(f32[128,128]{1,0:T(8,128)} %weight_ref.1) | copy-start | bytes 196612
  0.0 19.8 %copy-start.7 = (s32[1,1,8]{2,1,0:T(1,128)S(1)}, s32[1,1,8]{2,1,0:T(1,128)}, u32[]{:S(2)}) copy-start(s32[1,1,8]{2,1,0:T(1,128)} %list_ref.1) | copy-start | bytes 100
  1.1 19.6 %collective-permute-start = (bf16[5,8,1024]{2,1,0:T(8,128)(2,1)S(1)}, bf16[5,8,1024]{2,1,0:T(8,128)(2,1)S(1)}, u32[]{:S(2)}, u32[]{:S(2)}) collective-permute-start(bf16[5,8,1024]{2,1,0:T(8,128)(2,1)S(1)} %get-tuple-element.16), channel_id=1, source_target_pairs={{0,1},{2,3},{4,5},{6,7},{8,9},{10,11},{12,13},{14,15},{16,17},{18,... | collective-permute-start | bytes 245768 | tf_op jit(solution)/shard_map/ppermute | solution.py:244
  17.2 7.4 %collective-permute-start.1 = (bf16[5,8,1024]{2,1,0:T(8,128)(2,1)S(1)}, bf16[5,8,1024]{2,1,0:T(8,128)(2,1)S(1)}, u32[]{:S(2)}, u32[]{:S(2)}) collective-permute-start(bf16[5,8,1024]{2,1,0:T(8,128)(2,1)S(1)} %get-tuple-element.17), channel_id=1, source_target_pairs={{1,2},{3,4},{5,6},{7,8},{9,10},{11,12},{13,14},{15,16},{17,18},{19... | collective-permute-start | bytes 245768 | tf_op jit(solution)/shard_map/ppermute | solution.py:243
  24.5 10.5 %copy-start = (bf16[1024,1024]{1,0:T(8,128)(2,1)S(1)}, bf16[1024,1024]{1,0:T(8,128)(2,1)}, u32[]{:S(2)}) copy-start(bf16[1024,1024]{1,0:T(8,128)(2,1)} %w_mid_ref.1) | copy-start | bytes 6291460
  24.6 10.5 %copy-start.1 = (bf16[512,1024]{1,0:T(8,128)(2,1)S(1)}, bf16[512,1024]{1,0:T(8,128)(2,1)}, u32[]{:S(2)}) copy-start(bf16[512,1024]{1,0:T(8,128)(2,1)} %w_in_ref.1) | copy-start | bytes 3145732
  24.6 10.5 %copy-start.2 = (bf16[1024,512]{1,0:T(8,128)(2,1)S(1)}, bf16[1024,512]{1,0:T(8,128)(2,1)}, u32[]{:S(2)}) copy-start(bf16[1024,512]{1,0:T(8,128)(2,1)} %w_out_ref.1) | copy-start | bytes 3145732
